TPU v7x, 256 devices: a whole 4x4x8 slice. The times are simulated.
256 devices in a mesh: blk: 4 (over y_hi, core), dp: 64 (over z, x, y_lo).
Axes of the slice: x: 4, y: 4 (y_hi: 2, y_lo: 2; y = y_hi * 2 + y_lo), z: 8, core: 2. Of those that a mesh axis runs over, the one named last changes fastest.
Arguments:
- fingerprints: bfloat16 [98304, 2048], P(('blk', 'dp')), may hold values from 0 to 3, as said below
- w_first: bfloat16 [2048, 1024], replicated, may hold values from -0.3125 to 0.3125
- w_second: bfloat16 [1024, 512], replicated, may hold values from -0.0625 to 0.0625
Outputs:
- grad_first: float32 [2048, 1024], P('dp')
- grad_second: float32 [1024, 512], P('dp')
Inputs may be any that keep to these rules, and one draw needn't show every extreme that they name: `fingerprints`: Non-negative feature weights; every molecule has a third or more of its features nonzero.
All inputs are finite; a program needn't handle non-finite values.
Results may differ from a plain program's by a relative error of at most 0.003.
Values may be sent and summed in bfloat16 or wider, within the bound.
A program may use at most 64 MiB of HBM per device.

v0:
```python
import math

import jax
import jax.numpy as jnp
from jax import lax
from jax.sharding import PartitionSpec as P


def pair_tile(mine_feats, mine_embed, mine_sqn, other, width):
    other_feats = other[:, :width]
    other_embed = other[:, width:]
    other_sqn = jnp.sum(jnp.square(other_feats.astype(jnp.float32)), axis=1)
    contract = (((1,), (1,)), ((), ()))
    inter = lax.dot_general(mine_feats, other_feats, contract, preferred_element_type=jnp.float32)
    tanimoto = inter / (mine_sqn[:, None] + other_sqn[None, :] - inter)
    scale = 1.0 / math.sqrt(mine_embed.shape[1])
    pred = (
        lax.dot_general(mine_embed, other_embed, contract, preferred_element_type=jnp.float32)
        * scale
    )
    return ((pred - tanimoto).astype(jnp.bfloat16), other_embed)


def column_product(left, right):
    return lax.dot_general(
        left, right, (((0,), (0,)), ((), ())), preferred_element_type=jnp.float32
    )


def per_device(fingerprints, w_first, w_second):
    tok_rows, width = fingerprints.shape
    blk_count = lax.axis_size("blk")
    dp_count = lax.axis_size("dp")
    group_rows = tok_rows * blk_count
    all_rows = group_rows * dp_count
    pre = jnp.dot(fingerprints, w_first, preferred_element_type=jnp.float32)
    sig = jax.nn.sigmoid(pre)
    hidden = (pre * sig).astype(jnp.bfloat16)
    embed = jnp.dot(hidden, w_second, preferred_element_type=jnp.float32).astype(jnp.bfloat16)
    mine_sqn = jnp.sum(jnp.square(fingerprints.astype(jnp.float32)), axis=1)
    packed = jnp.concatenate([fingerprints, embed], axis=1)
    resid, other_embed = pair_tile(
        fingerprints, embed, mine_sqn, lax.all_gather(packed, "blk", axis=0, tiled=True), width
    )
    summed = jnp.dot(resid, other_embed, preferred_element_type=jnp.float32)
    dembed = (summed * (2.0 / math.sqrt(group_rows * all_rows))).astype(jnp.bfloat16)
    dhidden = lax.dot_general(
        dembed, w_second, (((1,), (1,)), ((), ())), preferred_element_type=jnp.float32
    )
    dpre = (dhidden * sig * (1.0 + pre * (1.0 - sig))).astype(jnp.bfloat16)
    first_part = lax.psum_scatter(
        column_product(fingerprints, dpre), "dp", scatter_dimension=0, tiled=True
    )
    second_part = lax.psum_scatter(
        column_product(hidden, dembed), "dp", scatter_dimension=0, tiled=True
    )
    grad_first, grad_second = lax.psum((first_part, second_part), "blk")
    return (grad_first, grad_second)


def solution(mesh):
    in_specs = (P(("blk", "dp"), None), P(), P())
    out_specs = (P("dp", None), P("dp", None))
    return jax.shard_map(
        per_device, mesh=mesh, in_specs=in_specs, out_specs=out_specs, check_vma=False
    )
```

profile of v0, /device:TPU:1, one launch (start us, length us, event | category | flops | bytes accessed | tf_op | source)
XLA Modules:
  0.0 816.7 jit_solution(17026861810282639801)
XLA Ops:
  7.2 0.0 copy-start
  7.2 0.0 all-gather.2.cloned.1.call-start
  7.2 4.5 fusion.22
  11.8 0.0 copy-start.2
  11.8 1.1 copy-done.2
  12.9 0.0 copy-done
  12.9 0.0 copy-start.1
  12.9 0.6 convolution_convert_fusion
  13.5 0.8 copy-done.1
  14.3 1.5 pad_maximum_fusion
  15.8 0.0 all-gather.2.cloned.1.call-update
  15.9 0.0 reduce-scatter.7.cloned.1.call-start
  15.9 0.4 multiply_reduce_fusion.1
  16.3 65.9 %all-gather.2.cloned.1.call-done = bf16[1536,2560]{1,0:T(8,128)(2,1)} async-done(((bf16[384,2560]{1,0:T(8,128)(2,1)}), bf16[1536,2560]{1,0:T(8,128)(2,1)}) %all-gather.2.cloned.1.call-update) | async-done | bytes 7864336 | tf_op jit(solution)/shard_map/all_gather | solution.py:43
  82.2 4.1 multiply_reduce_fusion
  86.2 7.7 fusion.3
  93.9 4.4 fusion.13
  98.4 6.5 convolution_bitcast_fusion
  104.9 9.3 %copy.7 = f32[2048,1024]{1,0:T(8,128)} copy(f32[2048,1024]{0,1:T(8,128)} %convolution_bitcast_fusion) | data formatting | bytes 16777216
  114.2 0.0 copy-start.3
  114.2 0.0 reduce-scatter.7.cloned.1.call-update
  114.2 0.0 reduce-scatter.5.cloned.1.call-start
  114.3 1.3 copy-done.3
  115.6 2.2 fusion.21
  117.8 0.0 reduce-scatter.5.cloned.1.call-update
  117.8 0.0 all-reduce.2.cloned.1.call-start
  117.9 283.1 %reduce-scatter.7.cloned.1.call-done = f32[32,1024]{1,0:T(8,128)} async-done(((f32[2048,1024]{1,0:T(8,128)}), f32[32,1024]{1,0:T(8,128)}) %reduce-scatter.7.cloned.1.call-update) | async-done | bytes 131088
  401.0 1.9 copy.8
  402.8 0.0 all-reduce.2.cloned.1.call-update
  402.9 309.9 %reduce-scatter.5.cloned.1.call-done = f32[16,512]{1,0:T(8,128)} async-done(((f32[1024,512]{1,0:T(8,128)}), f32[16,512]{1,0:T(8,128)}) %reduce-scatter.5.cloned.1.call-update) | async-done | bytes 32784 | tf_op jit(solution)/shard_map/reduce_scatter | solution.py:54
  712.7 63.9 %psum.15 = f32[16,512]{1,0:T(8,128)} all-reduce(f32[16,512]{1,0:T(8,128)} %reduce-scatter.5.cloned.1.call-done), channel_id=1, replica_groups=mesh['blk'=4,'dp'=64] {'blk'}, use_global_device_ids=true, to_apply=%region_5.0 | all-reduce | flops 8192 | bytes 65536 | tf_op jit(solution)/shard_map/psum | solution.py:57
  776.6 31.6 %all-reduce.2.cloned.1.call-done = f32[32,1024]{0,1:T(8,128)} async-done(((f32[32,1024]{0,1:T(8,128)}), f32[32,1024]{0,1:T(8,128)}) %all-reduce.2.cloned.1.call-update) | async-done | bytes 131088 | tf_op jit(solution)/shard_map/psum | solution.py:57
  808.3 1.9 copy.6
Async XLA Ops:
  7.2 5.8 copy-start
  7.2 75.0 %all-gather.2.cloned.1.call-start = ((), (), s32[]{:S(2)}) async-start(), calls=%async_computation.2 | async-start | bytes 9830400 | tf_op jit(solution)/shard_map/all_gather | solution.py:43
  11.8 1.2 copy-start.2
  12.9 1.4 copy-start.1
  15.9 385.1 %reduce-scatter.7.cloned.1.call-start = ((), (), s32[]{:S(2)}) async-start(), calls=%async_computation.5 | async-start | bytes 8519680
  114.2 1.4 copy-start.3
  114.2 598.5 %reduce-scatter.5.cloned.1.call-start = ((), (), s32[]{:S(2)}) async-start(), calls=%async_computation.4 | async-start | bytes 2129920 | tf_op jit(solution)/shard_map/reduce_scatter | solution.py:54
  117.8 690.5 %all-reduce.2.cloned.1.call-start = ((), (), s32[]{:S(2)}) async-start(), calls=%async_computation.3 | async-start | bytes 1048576 | tf_op jit(solution)/shard_map/psum | solution.py:57
Sparse Core Ops, SparseCore 0:
  16.0 66.1 all-gather.1
  114.3 286.5 reduce-scatter.6
  403.5 309.2 reduce-scatter.4
  715.4 92.7 all-reduce.1
where the time goes:
time: 817 us
  waiting for transfers between devices  691 us (85%)
  blocking collectives  63.9 us (8%)
  matrix products  26 us (3%)
  local copies, waits for them, and re-layouts  16.3 us (2%)
  between operations  13.8 us (2%)
    reduce_scatter x1, waiting for transfers between devices, per_device(): lax.psum_scatter(column_product(hidden, dembed), 'dp', scatter_dimension=...  310 us
    unnamed x5, waiting for transfers between devices  283 us
    all_gather x1, waiting for transfers between devices, per_device(): lax.all_gather(packed, 'blk', axis=0, tiled=True)  65.9 us
    psum x1, blocking collectives, per_device(): grad_first, grad_second = lax.psum((first_part, second_part), 'blk')  63.9 us
    psum x1, waiting for transfers between devices, per_device(): grad_first, grad_second = lax.psum((first_part, second_part), 'blk')  31.6 us
    unnamed x11, local copies, waits for them, and re-layouts  16.3 us
  transfers between devices with their start and end apart: 4, of which 4 were waited for; matrix products, arithmetic and copies ran while one was open for 1% of the time, Pallas kernels for 0%

commit v1 on v0

v1 whole, which is shorter than its diff:
```python
import functools
import math

import jax
import jax.numpy as jnp
from jax import lax
from jax.experimental import pallas as pl
from jax.experimental.pallas import tpu as pltpu
from jax.sharding import PartitionSpec as P

MESH = pl.DeviceIdType.MESH
F32 = jnp.float32
BF16 = jnp.bfloat16
NZ, NX = 8, 4
T = 256
HALF = 128


def dot_nt(a, b):
    return lax.dot_general(a, b, (((1,), (1,)), ((), ())), preferred_element_type=F32)


def dot_nn(a, b):
    return jnp.dot(a, b, preferred_element_type=F32)


def group_kernel(
    scale, fp_in, w1_in, w2_in, g1_out, g2_out,
    fp, fpt, w1, w2, hid, hidt, emb, summed, gate, demb, dpre, sqc, sqr,
    load_sem, send_sem, recv_sem, pass_send, pass_recv,
):
    blk = lax.axis_index("blk")
    tok, d_in = fp_in.shape
    width = w1_in.shape[1]
    half = 2 * tok
    pieces = tok // HALF
    groups = (4 * tok) // T
    local = half // T
    far = {"blk": (blk + 2) % 4}
    near = {"blk": (blk // 2) * 2 + 1 - blk % 2}

    barrier = pltpu.get_barrier_semaphore()
    for peer in (far, near):
        pl.semaphore_signal(barrier, inc=1, device_id=peer, device_id_type=MESH)
    loads = [
        pltpu.make_async_copy(fp_in, fp.at[pl.ds(0, tok)], load_sem.at[0]),
        pltpu.make_async_copy(w1_in, w1, load_sem.at[1]),
        pltpu.make_async_copy(w2_in, w2, load_sem.at[2]),
    ]
    for load in loads:
        load.start()
    pl.semaphore_wait(barrier, 2)

    def remote(src, dst, send, recv, peer):
        return pltpu.make_async_remote_copy(
            src_ref=src, dst_ref=dst, send_sem=send, recv_sem=recv,
            device_id=peer, device_id_type=MESH,
        )

    far_copies = [
        remote(
            fp_in.at[pl.ds(p * HALF, HALF)], fp.at[pl.ds(half + p * T, HALF)],
            send_sem.at[p], recv_sem.at[p], far,
        )
        for p in range(pieces)
    ]
    near_copy = remote(
        fp_in, fp.at[pl.ds(tok, tok)], send_sem.at[pieces], recv_sem.at[pieces], near
    )
    for copy in far_copies:
        copy.start()
    near_copy.start()

    def passing(p):
        return remote(
            fp.at[pl.ds(half + p * T, HALF)], fp.at[pl.ds(half + p * T + HALF, HALF)],
            pass_send.at[p], pass_recv.at[p], near,
        )

    summed[...] = jnp.zeros_like(summed)
    for load in loads:
        load.wait()

    def encode(p):
        rows = pl.ds(p * T, T)

        @pl.loop(0, width // T)
        def _(n):
            cols = pl.ds(pl.multiple_of(n * T, T), T)
            pre = dot_nn(fp[rows, :], w1[:, cols])
            sig = 1.0 / (1.0 + jnp.exp(-pre))
            h = (pre * sig).astype(BF16)
            hid[:, cols] = h
            hidt[cols, rows] = h.T

            @pl.when(n == blk)
            def _():
                gate[rows, :] = sig * (1.0 + pre * (1.0 - sig))

        emb[rows, :] = dot_nn(hid[...], w2[...]).astype(BF16)

        @pl.loop(0, d_in // T)
        def _(n):
            cols = pl.ds(pl.multiple_of(n * T, T), T)
            fpt[cols, rows] = fp[rows, cols].T

    def residual(i, p, inter):
        den = sqc[pl.ds(i * T, T), :][:, :1] + sqr[:1, pl.ds(p * T, T)] - inter
        pred = dot_nt(emb[pl.ds(i * T, T), :], emb[pl.ds(p * T, T), :])
        return (pred * (1.0 / math.sqrt(emb.shape[1])) - inter / den).astype(BF16)

    def pairs(p):
        rows = pl.ds(p * T, T)
        inter = dot_nt(fp[rows, :], fp[rows, :])
        r_id = lax.broadcasted_iota(jnp.int32, (T, T), 0)
        c_id = lax.broadcasted_iota(jnp.int32, (T, T), 1)
        diag = jnp.where(r_id == c_id, inter, 0.0)
        sqc[rows, :] = jnp.broadcast_to(jnp.sum(diag, axis=1, keepdims=True), (T, 128))
        sqr[:, rows] = jnp.broadcast_to(jnp.sum(diag, axis=0, keepdims=True), (8, T))
        resid = residual(p, p, inter)
        summed[rows, :] += dot_nn(resid, emb[rows, :])

        def other(i, carry):
            above = pl.ds(pl.multiple_of(i * T, T), T)
            resid = residual(i, p, dot_nt(fp[above, :], fp[rows, :]))
            summed[above, :] += dot_nn(resid, emb[rows, :])
            summed[rows, :] += dot_nn(resid.T, emb[above, :])
            return carry

        lax.fori_loop(0, p, other, 0)

    @pl.loop(0, groups)
    def _(p):
        p = jnp.int32(p)

        @pl.when(p == 1)
        def _():
            near_copy.wait()

        for k in range(pieces):

            @pl.when(p == local + k)
            def _(k=k):
                far_copies[k].wait()
                passing(k).start()
                passing(k).wait()

        encode(pl.multiple_of(p, 1))
        pairs(pl.multiple_of(p, 1))

    demb[...] = (summed[...] * scale).astype(BF16)

    @pl.loop(0, groups)
    def _(i):
        rows = pl.ds(pl.multiple_of(i * T, T), T)
        back = dot_nt(demb[rows, :], w2[pl.ds(pl.multiple_of(blk * T, T), T), :])
        dpre[rows, :] = (back * gate[rows, :]).astype(BF16)

    @pl.loop(0, NZ)
    def _(z):
        step = d_in // NZ
        part = dot_nn(fpt[pl.ds(pl.multiple_of(z * step, step), step), :], dpre[...])
        sub = step // NX
        for x in range(NX):
            g1_out[x, pl.ds(pl.multiple_of(z * sub, sub), sub), :] = part[
                x * sub : (x + 1) * sub
            ].astype(BF16)
        cols = demb.shape[1] // 4
        step = width // NZ
        part = dot_nn(
            hidt[pl.ds(pl.multiple_of(z * step, step), step), :],
            demb[:, pl.ds(pl.multiple_of(blk * cols, cols), cols)],
        )
        sub = step // NX
        for x in range(NX):
            g2_out[x, pl.ds(pl.multiple_of(z * sub, sub), sub), :] = part[
                x * sub : (x + 1) * sub
            ].astype(BF16)


def group_gradients(fingerprints, w_first, w_second, scale):
    tok, d_in = fingerprints.shape
    hidden, width = w_second.shape
    rows = 4 * tok
    pieces = tok // HALF
    any_spec = pl.BlockSpec(memory_space=pl.ANY)
    vmem_spec = pl.BlockSpec(memory_space=pltpu.VMEM)
    return pl.pallas_call(
        functools.partial(group_kernel, scale),
        out_shape=(
            jax.ShapeDtypeStruct((NX, d_in // NX, hidden // 4), BF16),
            jax.ShapeDtypeStruct((NX, hidden // NX, width // 4), BF16),
        ),
        in_specs=[any_spec] * 3,
        out_specs=(vmem_spec, vmem_spec),
        scratch_shapes=[
            pltpu.VMEM((rows, d_in), BF16),
            pltpu.VMEM((d_in, rows), BF16),
            pltpu.VMEM((d_in, hidden), BF16),
            pltpu.VMEM((hidden, width), BF16),
            pltpu.VMEM((T, hidden), BF16),
            pltpu.VMEM((hidden, rows), BF16),
            pltpu.VMEM((rows, width), BF16),
            pltpu.VMEM((rows, width), F32),
            pltpu.VMEM((rows, hidden // 4), F32),
            pltpu.VMEM((rows, width), BF16),
            pltpu.VMEM((rows, hidden // 4), BF16),
            pltpu.VMEM((rows, 128), F32),
            pltpu.VMEM((8, rows), F32),
            pltpu.SemaphoreType.DMA((3,)),
            pltpu.SemaphoreType.DMA((pieces + 1,)),
            pltpu.SemaphoreType.DMA((pieces + 1,)),
            pltpu.SemaphoreType.DMA((pieces,)),
            pltpu.SemaphoreType.DMA((pieces,)),
        ],
        compiler_params=pltpu.CompilerParams(
            collective_id=0, has_side_effects=True, vmem_limit_bytes=56 << 20
        ),
        name="group_gradients",
    )(fingerprints, w_first, w_second)


def reduce_kernel(
    g1, g2, o1, o2, own1, own2, xb1, xb2, zs1, zs2, zb1, zb2, ys1, ys2, yb1, yb2,
    load_sem, xs, xr, zs, zr, ys, yr,
):
    blk = lax.axis_index("blk")
    dp = lax.axis_index("dp")
    z, x = dp // 8, (dp // 2) % 4
    y, c = (blk // 2) * 2 + dp % 2, blk % 2

    def at(z, x, y, c):
        return {"blk": (y // 2) * 2 + c, "dp": (z * NX + x) * 2 + y % 2}

    x_peers = [at(z, (x + k) % NX, y, c) for k in range(1, NX)]
    z_peers = [at((z + k) % NZ, x, y, c) for k in range(1, NZ)]
    y_steps = [(dy, dc) for dy in range(4) for dc in range(2)][1:]
    y_peers = [at(z, x, (y + dy) % 4, (c + dc) % 2) for dy, dc in y_steps]
    barrier = pltpu.get_barrier_semaphore()
    for peer in x_peers + z_peers + y_peers:
        pl.semaphore_signal(barrier, inc=1, device_id=peer, device_id_type=MESH)
    loads = [
        pltpu.make_async_copy(g1.at[x], own1, load_sem.at[0]),
        pltpu.make_async_copy(g2.at[x], own2, load_sem.at[1]),
    ]
    for load in loads:
        load.start()
    pl.semaphore_wait(barrier, len(x_peers) + len(z_peers) + len(y_peers))

    def remote(src, dst, send, recv, peer):
        return pltpu.make_async_remote_copy(
            src_ref=src, dst_ref=dst, send_sem=send, recv_sem=recv,
            device_id=peer, device_id_type=MESH,
        )

    copies = []
    for k in (2, 1, 3):
        peer, to = x_peers[k - 1], (x + k) % NX
        copies.append(remote(g1.at[to], xb1.at[k - 1], xs.at[0, k - 1], xr.at[0, k - 1], peer))
        copies.append(remote(g2.at[to], xb2.at[k - 1], xs.at[1, k - 1], xr.at[1, k - 1], peer))
    for copy in copies:
        copy.start()
    for load in loads:
        load.wait()
    for copy in copies:
        copy.wait()

    def sum_x(own, buf):
        total = own[...].astype(F32)
        for k in range(NX - 1):
            total = total + buf[k].astype(F32)
        return total

    zs1[...] = sum_x(own1, xb1).astype(BF16).reshape(zs1.shape)
    zs2[...] = sum_x(own2, xb2).astype(BF16).reshape(zs2.shape)

    copies = []
    for k in (4, 3, 5, 2, 6, 1, 7):
        peer, to = z_peers[k - 1], (z + k) % NZ
        copies.append(remote(zs1.at[to], zb1.at[k - 1], zs.at[0, k - 1], zr.at[0, k - 1], peer))
        copies.append(remote(zs2.at[to], zb2.at[k - 1], zs.at[1, k - 1], zr.at[1, k - 1], peer))
    for copy in copies:
        copy.start()
    for copy in copies:
        copy.wait()

    def sum_z(own, buf):
        total = own[z].astype(F32)
        for k in range(NZ - 1):
            total = total + buf[k].astype(F32)
        return total

    ys1[...] = sum_z(zs1, zb1).reshape(ys1.shape)
    ys2[...] = sum_z(zs2, zb2).reshape(ys2.shape)

    copies = []
    for k, (dy, dc) in enumerate(y_steps):
        peer, to = y_peers[k], (y + dy) % 2
        slot = y * 2 + c
        copies.append(remote(ys1.at[to], yb1.at[slot], ys.at[0, k], yr.at[0, k], peer))
        copies.append(remote(ys2.at[to], yb2.at[slot], ys.at[1, k], yr.at[1, k], peer))
    for copy in copies:
        copy.start()
    yb1[y * 2 + c] = ys1[y % 2]
    yb2[y * 2 + c] = ys2[y % 2]
    for copy in copies:
        copy.wait()
    for h in range(2):
        for core in range(2):
            quarter = 2 * h + core
            low, high = 4 * h + core, 4 * h + 2 + core
            o1[:, quarter * o1.shape[1] // 4 : (quarter + 1) * o1.shape[1] // 4] = (
                yb1[low] + yb1[high]
            )
            o2[:, quarter * o2.shape[1] // 4 : (quarter + 1) * o2.shape[1] // 4] = (
                yb2[low] + yb2[high]
            )


def reduce_gradients(g1, g2):
    vmem_spec = pl.BlockSpec(memory_space=pltpu.VMEM)
    any_spec = pl.BlockSpec(memory_space=pl.ANY)
    _, r1, c1 = g1.shape
    _, r2, c2 = g2.shape
    z1, z2 = r1 // NZ, r2 // NZ
    return pl.pallas_call(
        reduce_kernel,
        out_shape=(
            jax.ShapeDtypeStruct((z1 // 2, 4 * c1), F32),
            jax.ShapeDtypeStruct((z2 // 2, 4 * c2), F32),
        ),
        in_specs=[any_spec] * 2,
        out_specs=(vmem_spec, vmem_spec),
        scratch_shapes=[
            pltpu.VMEM((r1, c1), BF16),
            pltpu.VMEM((r2, c2), BF16),
            pltpu.VMEM((NX - 1, r1, c1), BF16),
            pltpu.VMEM((NX - 1, r2, c2), BF16),
            pltpu.VMEM((NZ, z1, c1), BF16),
            pltpu.VMEM((NZ, z2, c2), BF16),
            pltpu.VMEM((NZ - 1, z1, c1), BF16),
            pltpu.VMEM((NZ - 1, z2, c2), BF16),
            pltpu.VMEM((2, z1 // 2, c1), F32),
            pltpu.VMEM((2, z2 // 2, c2), F32),
            pltpu.VMEM((8, z1 // 2, c1), F32),
            pltpu.VMEM((8, z2 // 2, c2), F32),
            pltpu.SemaphoreType.DMA((2,)),
            pltpu.SemaphoreType.DMA((2, NX - 1)),
            pltpu.SemaphoreType.DMA((2, NX - 1)),
            pltpu.SemaphoreType.DMA((2, NZ - 1)),
            pltpu.SemaphoreType.DMA((2, NZ - 1)),
            pltpu.SemaphoreType.DMA((2, 7)),
            pltpu.SemaphoreType.DMA((2, 7)),
        ],
        compiler_params=pltpu.CompilerParams(
            collective_id=1, has_side_effects=True, vmem_limit_bytes=40 << 20
        ),
        name="reduce_gradients",
    )(g1, g2)


def per_device(fingerprints, w_first, w_second):
    group_rows = fingerprints.shape[0] * lax.axis_size("blk")
    all_rows = group_rows * lax.axis_size("dp")
    scale = 2.0 / math.sqrt(group_rows * all_rows)
    g1, g2 = group_gradients(fingerprints, w_first, w_second, scale)
    return reduce_gradients(g1, g2)


def solution(mesh):
    in_specs = (P(("blk", "dp"), None), P(), P())
    out_specs = (P("dp", None), P("dp", None))
    return jax.shard_map(
        per_device, mesh=mesh, in_specs=in_specs, out_specs=out_specs, check_vma=False
    )
```

time: 817 us -> 104 us (0.13)
  waiting for transfers between devices: 691 us -> 0 us
  Pallas kernels: 0 us -> 100 us
  blocking collectives: 63.9 us -> 0 us
  matrix products: 26 us -> 0 us
  between operations: 13.8 us -> 0.66 us
  local copies, waits for them, and re-layouts: 16.3 us -> 3.44 us
    reduce_scatter x1 -> x0, waiting for transfers between devices: 310 us -> none  [per_device(): lax.psum_scatter(column_product(hidden, dembed), 'dp', scatter_dimension=...]
    unnamed x5 -> x0, waiting for transfers between devices: 283 us -> none
    pallas_call x0 -> x2, Pallas kernels: none -> 100 us  [the longest x1 60.7 us: group_gradients(): pl.pallas_call(functools.partial(group_kernel, scale), out_shape=(jax.Sha...]
    all_gather x1 -> x0, waiting for transfers between devices: 65.9 us -> none  [per_device(): lax.all_gather(packed, 'blk', axis=0, tiled=True)]
    psum x1 -> x0, blocking collectives: 63.9 us -> none  [per_device(): grad_first, grad_second = lax.psum((first_part, second_part), 'blk')]
    psum x1 -> x0, waiting for transfers between devices: 31.6 us -> none  [per_device(): grad_first, grad_second = lax.psum((first_part, second_part), 'blk')]
    dot_general x6 -> x0, matrix products: 26 us -> none  [the longest x2 8.73 us: column_product(): lax.dot_general(left, right, (((0,), (0,)), ((), ())), preferred_element_...]
    unnamed x11 -> x6, local copies, waits for them, and re-layouts: 16.3 us -> 3.44 us
  transfers between devices with their start and end apart: 4 -> 0, of which waited for: 4 -> 0; matrix products, arithmetic and copies ran while one was open for 1% -> 0% of each run, Pallas kernels for 0% -> 0%
where the time goes in v1:
time: 104 us
  Pallas kernels  100 us (96%)
  local copies, waits for them, and re-layouts  3.44 us (3%)
    pallas_call x1, Pallas kernels, group_gradients(): pl.pallas_call(functools.partial(group_kernel, scale), out_shape=(jax.Sha...  60.7 us
    pallas_call x1, Pallas kernels, reduce_gradients(): pl.pallas_call(reduce_kernel, out_shape=(jax.ShapeDtypeStruct((z1 // 2, 4...  39.3 us
    unnamed x6, local copies, waits for them, and re-layouts  3.44 us

profile of v1, /device:TPU:1, one launch (start us, length us, event | category | flops | bytes accessed | tf_op | source)
XLA Modules:
  0.0 104.1 jit_solution(9360559527482619496)
XLA Ops:
  0.6 60.7 %group_gradients.1 = (bf16[4,512,256]{2,1,0:T(8,128)(2,1)}, bf16[4,256,128]{2,1,0:T(8,128)(2,1)}) custom-call(bf16[384,2048]{1,0:T(8,128)(2,1)} %fp_in.1, bf16[2048,1024]{1,0:T(8,128)(2,1)} %w1_in.1, bf16[1024,512]{1,0:T(8,128)(2,1)} %w2_in.1), custom_call_target="tpu_custom_call" | custom-call | tf_op jit(solution)/shard_map/group_gradients/pallas_call | solution.py:188
  61.3 0.0 copy-start
  61.3 1.2 %copy-done = bf16[4,512,256]{2,1,0:T(8,128)(2,1)S(1)} copy-done((bf16[4,512,256]{2,1,0:T(8,128)(2,1)S(1)}, bf16[4,512,256]{2,1,0:T(8,128)(2,1)}, u32[]{:S(2)}) %copy-start) | copy-done | bytes 1048600
  62.5 0.0 copy-start.1
  62.5 0.9 copy-done.1
  63.5 39.3 %reduce_gradients.1 = (f32[32,1024]{1,0:T(8,128)S(1)}, f32[16,512]{1,0:T(8,128)S(1)}) custom-call(bf16[4,512,256]{2,1,0:T(8,128)(2,1)S(1)} %copy-done, bf16[4,256,128]{2,1,0:T(8,128)(2,1)S(1)} %copy-done.1), custom_call_target="tpu_custom_call" | custom-call | tf_op jit(solution)/shard_map/reduce_gradients/pallas_call | solution.py:326
  102.8 0.7 copy.7
  103.5 0.6 copy.8
Async XLA Ops:
  61.3 1.2 %copy-start = (bf16[4,512,256]{2,1,0:T(8,128)(2,1)S(1)}, bf16[4,512,256]{2,1,0:T(8,128)(2,1)}, u32[]{:S(2)}) copy-start(bf16[4,512,256]{2,1,0:T(8,128)(2,1)} %get-tuple-element.4.g1) | copy-start | bytes 3145732
  62.5 0.9 copy-start.1

commit v2 on v0

v2 whole, which is shorter than its diff:
```python
import functools
import math

import jax
import jax.numpy as jnp
from jax import lax
from jax.experimental import pallas as pl
from jax.experimental.pallas import tpu as pltpu
from jax.sharding import PartitionSpec as P

MESH = pl.DeviceIdType.MESH
F32 = jnp.float32
BF16 = jnp.bfloat16
NZ, NX = 8, 4
T = 256
HALF = 128


def dot_nt(a, b):
    return lax.dot_general(a, b, (((1,), (1,)), ((), ())), preferred_element_type=F32)


def dot_nn(a, b):
    return jnp.dot(a, b, preferred_element_type=F32)


def step_kernel(
    scale, fp_in, w1_in, w2_in, o1, o2,
    fp, fpt, w1, w2, hid, hidt, emb, summed, gate, demb, dpre, sqc, sqr,
    xo1, xo2, xb1, xb2, zs1, zs2, zb1, zb2, ys1, ys2, yb1, yb2,
    load_sem, send_sem, recv_sem, pass_send, pass_recv, xs, xr, zs, zr, ys, yr,
):
    blk = lax.axis_index("blk")
    dp = lax.axis_index("dp")
    z, x = dp // 8, (dp // 2) % 4
    y, c = (blk // 2) * 2 + dp % 2, blk % 2
    tok, d_in = fp_in.shape
    hidden, width = w2_in.shape
    half = 2 * tok
    rows_all = 4 * tok
    pieces = tok // HALF
    norm = 1.0 / math.sqrt(width)

    def at(z, x, y, c):
        return {"blk": (y // 2) * 2 + c, "dp": (z * NX + x) * 2 + y % 2}

    far = at(z, x, (y + 2) % 4, c)
    near = at(z, x, y, 1 - c)
    x_peers = [at(z, (x + k) % NX, y, c) for k in range(1, NX)]
    z_peers = [at((z + k) % NZ, x, y, c) for k in range(1, NZ)]
    y_steps = [(dy, dc) for dy in range(4) for dc in range(2)][1:]
    y_peers = [at(z, x, (y + dy) % 4, (c + dc) % 2) for dy, dc in y_steps]

    barrier = pltpu.get_barrier_semaphore()
    for peer in y_peers + x_peers + z_peers:
        pl.semaphore_signal(barrier, inc=1, device_id=peer, device_id_type=MESH)
    loads = [
        pltpu.make_async_copy(fp_in, fp.at[pl.ds(0, tok)], load_sem.at[0]),
        pltpu.make_async_copy(w1_in, w1, load_sem.at[1]),
        pltpu.make_async_copy(w2_in, w2, load_sem.at[2]),
    ]
    for load in loads:
        load.start()
    pl.semaphore_wait(barrier, len(x_peers) + len(z_peers) + len(y_peers))

    def remote(src, dst, send, recv, peer):
        return pltpu.make_async_remote_copy(
            src_ref=src, dst_ref=dst, send_sem=send, recv_sem=recv,
            device_id=peer, device_id_type=MESH,
        )

    def far_copy(p):
        return remote(
            fp_in.at[pl.ds(p * HALF, HALF)], fp.at[pl.ds(half + p * T, HALF)],
            send_sem.at[p], recv_sem.at[p], far,
        )

    def passing(p):
        return remote(
            fp.at[pl.ds(half + p * T, HALF)], fp.at[pl.ds(half + p * T + HALF, HALF)],
            pass_send.at[p], pass_recv.at[p], near,
        )

    near_copy = remote(
        fp_in, fp.at[pl.ds(tok, tok)], send_sem.at[pieces], recv_sem.at[pieces], near
    )
    for p in range(pieces):
        far_copy(p).start()
    near_copy.start()
    for load in loads:
        load.wait()
    near_copy.wait()

    def encode_columns(rows, cols):
        pre = dot_nn(fp[rows, :], w1[:, cols])
        sig = 1.0 / (1.0 + jnp.exp(-pre))
        h = (pre * sig).astype(BF16)
        hid[pl.ds(0, h.shape[0]), cols] = h
        hidt[cols, rows] = h.T
        gate[rows, cols] = sig * (1.0 + pre * (1.0 - sig))

    def embed(rows, count):
        emb[rows, :] = dot_nn(hid[pl.ds(0, count), :], w2[...]).astype(BF16)

    def residual(upper, lower):
        inter = dot_nt(fp[upper, :], fp[lower, :])
        den = sqc[upper, :][:, :1] + sqr[:1, lower] - inter
        pred = dot_nt(emb[upper, :], emb[lower, :])
        return (pred * norm - inter / den).astype(BF16)

    def diagonal(rows):
        inter = dot_nt(fp[rows, :], fp[rows, :])
        r_id = lax.broadcasted_iota(jnp.int32, (T, T), 0)
        c_id = lax.broadcasted_iota(jnp.int32, (T, T), 1)
        diag = jnp.where(r_id == c_id, inter, 0.0)
        col = jnp.sum(diag, axis=1, keepdims=True)
        row = jnp.sum(diag, axis=0, keepdims=True)
        sqc[rows, :] = jnp.broadcast_to(col, (T, 128))
        sqr[:, rows] = jnp.broadcast_to(row, (8, T))
        pred = dot_nt(emb[rows, :], emb[rows, :])
        resid = (pred * norm - inter / (col + row - inter)).astype(BF16)
        return dot_nn(resid, emb[rows, :])

    def cross(upper, lower):
        resid = residual(upper, lower)
        summed[upper, :] += dot_nn(resid, emb[lower, :])
        summed[lower, :] += dot_nn(resid.T, emb[upper, :])

    @pl.loop(0, hidden // T)
    def _(n):
        cols = pl.ds(pl.multiple_of(n * T, T), T)
        encode_columns(pl.ds(0, half), cols)

    @pl.loop(0, d_in // T)
    def _(n):
        cols = pl.ds(pl.multiple_of(n * T, T), T)
        fpt[cols, pl.ds(0, half)] = fp[pl.ds(0, half), cols].T

    embed(pl.ds(0, half), half)
    for r in range(0, half, T):
        summed[pl.ds(r, T), :] = diagonal(pl.ds(r, T))
        if r:
            cross(pl.ds(0, r), pl.ds(r, T))

    @pl.loop(0, pieces)
    def _(p):
        rows = pl.ds(pl.multiple_of(half + p * T, T), T)
        far_copy(p).wait()
        passing(p).start()
        passing(p).wait()
        for n in range(0, hidden, T):
            encode_columns(rows, pl.ds(n, T))
        for n in range(0, d_in, T):
            fpt[pl.ds(n, T), rows] = fp[rows, pl.ds(n, T)].T
        embed(rows, T)
        summed[rows, :] = diagonal(rows)
        cross(pl.ds(0, half), rows)

        @pl.loop(0, p)
        def _(i):
            cross(pl.ds(pl.multiple_of(half + i * T, T), T), rows)

    demb[...] = (summed[...] * scale).astype(BF16)
    quarter = pl.ds(pl.multiple_of(blk * T, T), T)
    for r in range(0, rows_all, 2 * T):
        rows = pl.ds(r, 2 * T)
        back = dot_nt(demb[rows, :], w2[quarter, :])
        dpre[rows, :] = (back * gate[rows, quarter]).astype(BF16)

    def scatter_x(part, out, z0, step):
        sub = step // NX
        for k in range(part.shape[0] // step):
            for xx in range(NX):
                out[xx, pl.ds((z0 + k) * sub, sub), :] = part[
                    k * step + xx * sub : k * step + (xx + 1) * sub
                ].astype(BF16)

    def send_x(src, dst, sems):
        for k in (2, 1, 3):
            to = (x + k) % NX
            copy = remote(
                src(to), dst(k - 1), xs.at[sems, k - 1], xr.at[sems, k - 1], x_peers[k - 1]
            )
            copies.append(copy)
            copy.start()

    copies = []
    for part in range(2):
        span = d_in // 2
        scatter_x(
            dot_nn(fpt[pl.ds(part * span, span), :], dpre[...]),
            xo1, part * NZ // 2, d_in // NZ,
        )
        lines = pl.ds(part * span // NX, span // NX)
        send_x(lambda to: xo1.at[to, lines], lambda k: xb1.at[k, lines], part)
    cols = width // 4
    scatter_x(
        dot_nn(hidt[...], demb[:, pl.ds(pl.multiple_of(blk * cols, cols), cols)]),
        xo2, 0, hidden // NZ,
    )
    send_x(lambda to: xo2.at[to], lambda k: xb2.at[k], 2)
    for copy in copies:
        copy.wait()

    def sum_x(own, buf):
        total = own[x].astype(F32)
        for k in range(NX - 1):
            total = total + buf[k].astype(F32)
        return total

    zs1[...] = sum_x(xo1, xb1).astype(BF16).reshape(zs1.shape)
    zs2[...] = sum_x(xo2, xb2).astype(BF16).reshape(zs2.shape)

    copies = []
    for k in (4, 3, 5, 2, 6, 1, 7):
        peer, to = z_peers[k - 1], (z + k) % NZ
        copies.append(remote(zs1.at[to], zb1.at[k - 1], zs.at[0, k - 1], zr.at[0, k - 1], peer))
        copies.append(remote(zs2.at[to], zb2.at[k - 1], zs.at[1, k - 1], zr.at[1, k - 1], peer))
    for copy in copies:
        copy.start()
    for copy in copies:
        copy.wait()

    def sum_z(own, buf):
        total = own[z].astype(F32)
        for k in range(NZ - 1):
            total = total + buf[k].astype(F32)
        return total

    ys1[...] = sum_z(zs1, zb1).reshape(ys1.shape)
    ys2[...] = sum_z(zs2, zb2).reshape(ys2.shape)

    copies = []
    for k, (dy, dc) in enumerate(y_steps):
        peer, to = y_peers[k], (y + dy) % 2
        slot = y * 2 + c
        copies.append(remote(ys1.at[to], yb1.at[slot], ys.at[0, k], yr.at[0, k], peer))
        copies.append(remote(ys2.at[to], yb2.at[slot], ys.at[1, k], yr.at[1, k], peer))
    for copy in copies:
        copy.start()
    yb1[y * 2 + c] = ys1[y % 2]
    yb2[y * 2 + c] = ys2[y % 2]
    for copy in copies:
        copy.wait()
    for h in range(2):
        for core in range(2):
            q = 2 * h + core
            low, high = 4 * h + core, 4 * h + 2 + core
            o1[:, q * o1.shape[1] // 4 : (q + 1) * o1.shape[1] // 4] = yb1[low] + yb1[high]
            o2[:, q * o2.shape[1] // 4 : (q + 1) * o2.shape[1] // 4] = yb2[low] + yb2[high]


def gradients(fingerprints, w_first, w_second, scale):
    tok, d_in = fingerprints.shape
    hidden, width = w_second.shape
    rows = 4 * tok
    pieces = tok // HALF
    any_spec = pl.BlockSpec(memory_space=pl.ANY)
    vmem_spec = pl.BlockSpec(memory_space=pltpu.VMEM)
    r1, c1 = d_in // NX, hidden // 4
    r2, c2 = hidden // NX, width // 4
    z1, z2 = r1 // NZ, r2 // NZ
    dma = pltpu.SemaphoreType.DMA
    return pl.pallas_call(
        functools.partial(step_kernel, scale),
        out_shape=(
            jax.ShapeDtypeStruct((z1 // 2, 4 * c1), F32),
            jax.ShapeDtypeStruct((z2 // 2, 4 * c2), F32),
        ),
        in_specs=[any_spec] * 3,
        out_specs=(vmem_spec, vmem_spec),
        scratch_shapes=[
            pltpu.VMEM((rows, d_in), BF16),
            pltpu.VMEM((d_in, rows), BF16),
            pltpu.VMEM((d_in, hidden), BF16),
            pltpu.VMEM((hidden, width), BF16),
            pltpu.VMEM((2 * tok, hidden), BF16),
            pltpu.VMEM((hidden, rows), BF16),
            pltpu.VMEM((rows, width), BF16),
            pltpu.VMEM((rows, width), F32),
            pltpu.VMEM((rows, hidden), F32),
            pltpu.VMEM((rows, width), BF16),
            pltpu.VMEM((rows, hidden // 4), BF16),
            pltpu.VMEM((rows, 128), F32),
            pltpu.VMEM((8, rows), F32),
            pltpu.VMEM((NX, r1, c1), BF16),
            pltpu.VMEM((NX, r2, c2), BF16),
            pltpu.VMEM((NX - 1, r1, c1), BF16),
            pltpu.VMEM((NX - 1, r2, c2), BF16),
            pltpu.VMEM((NZ, z1, c1), BF16),
            pltpu.VMEM((NZ, z2, c2), BF16),
            pltpu.VMEM((NZ - 1, z1, c1), BF16),
            pltpu.VMEM((NZ - 1, z2, c2), BF16),
            pltpu.VMEM((2, z1 // 2, c1), F32),
            pltpu.VMEM((2, z2 // 2, c2), F32),
            pltpu.VMEM((8, z1 // 2, c1), F32),
            pltpu.VMEM((8, z2 // 2, c2), F32),
            dma((3,)),
            dma((pieces + 1,)),
            dma((pieces + 1,)),
            dma((pieces,)),
            dma((pieces,)),
            dma((3, NX - 1)),
            dma((3, NX - 1)),
            dma((2, NZ - 1)),
            dma((2, NZ - 1)),
            dma((2, 7)),
            dma((2, 7)),
        ],
        compiler_params=pltpu.CompilerParams(
            collective_id=0, has_side_effects=True, vmem_limit_bytes=60 << 20
        ),
        name="gradients",
    )(fingerprints, w_first, w_second)


def per_device(fingerprints, w_first, w_second):
    group_rows = fingerprints.shape[0] * lax.axis_size("blk")
    all_rows = group_rows * lax.axis_size("dp")
    scale = 2.0 / math.sqrt(group_rows * all_rows)
    return gradients(fingerprints, w_first, w_second, scale)


def solution(mesh):
    in_specs = (P(("blk", "dp"), None), P(), P())
    out_specs = (P("dp", None), P("dp", None))
    return jax.shard_map(
        per_device, mesh=mesh, in_specs=in_specs, out_specs=out_specs, check_vma=False
    )
```

time: 817 us -> 93.8 us (0.11)
  waiting for transfers between devices: 691 us -> 0 us
  Pallas kernels: 0 us -> 90 us
  blocking collectives: 63.9 us -> 0 us
  matrix products: 26 us -> 0 us
  local copies, waits for them, and re-layouts: 16.3 us -> 2.94 us
  between operations: 13.8 us -> 0.64 us
    reduce_scatter x1 -> x0, waiting for transfers between devices: 310 us -> none  [per_device(): lax.psum_scatter(column_product(hidden, dembed), 'dp', scatter_dimension=...]
    unnamed x5 -> x0, waiting for transfers between devices: 283 us -> none
    pallas_call x0 -> x1, Pallas kernels: none -> 90 us  [gradients(): pl.pallas_call(functools.partial(step_kernel, scale), out_shape=(jax.Shap...]
    all_gather x1 -> x0, waiting for transfers between devices: 65.9 us -> none  [per_device(): lax.all_gather(packed, 'blk', axis=0, tiled=True)]
    psum x1 -> x0, blocking collectives: 63.9 us -> none  [per_device(): grad_first, grad_second = lax.psum((first_part, second_part), 'blk')]
    psum x1 -> x0, waiting for transfers between devices: 31.6 us -> none  [per_device(): grad_first, grad_second = lax.psum((first_part, second_part), 'blk')]
    dot_general x6 -> x0, matrix products: 26 us -> none  [the longest x2 8.73 us: column_product(): lax.dot_general(left, right, (((0,), (0,)), ((), ())), preferred_element_...]
    unnamed x11 -> x2, local copies, waits for them, and re-layouts: 16.3 us -> 2.94 us
  transfers between devices with their start and end apart: 4 -> 0, of which waited for: 4 -> 0; matrix products, arithmetic and copies ran while one was open for 1% -> 0% of each run, Pallas kernels for 0% -> 0%
where the time goes in v2:
time: 93.8 us; the launch traced here: 93.6 us
  Pallas kernels  90 us (96%)
  local copies, waits for them, and re-layouts  2.94 us (3%)
    pallas_call x1, Pallas kernels, gradients(): pl.pallas_call(functools.partial(step_kernel, scale), out_shape=(jax.Shap...  90 us
    unnamed x2, local copies, waits for them, and re-layouts  2.94 us

profile of v2, /device:TPU:1, one launch (start us, length us, event | category | flops | bytes accessed | tf_op | source)
XLA Modules:
  0.0 93.6 jit_solution(18029292972860766855)
XLA Ops:
  0.6 90.0 %gradients.1 = (f32[32,1024]{1,0:T(8,128)}, f32[16,512]{1,0:T(8,128)}) custom-call(bf16[384,2048]{1,0:T(8,128)(2,1)} %fp_in.1, bf16[2048,1024]{1,0:T(8,128)(2,1)} %w1_in.1, bf16[1024,512]{1,0:T(8,128)(2,1)} %w2_in.1), custom_call_target="tpu_custom_call" | custom-call | tf_op jit(solution)/shard_map/gradients/pallas_call | solution.py:264
  90.7 1.6 %copy.7 = f32[32,1024]{1,0:T(8,128)} copy(f32[32,1024]{1,0:T(8,128)} %get-tuple-element.4) | data formatting | bytes 262144
  92.2 1.4 %copy.8 = f32[16,512]{1,0:T(8,128)} copy(f32[16,512]{1,0:T(8,128)} %get-tuple-element.5) | data formatting | bytes 65536

commit v3 on v2

--- a/solution.py
+++ b/solution.py
@@ -27,8 +27,9 @@
 def step_kernel(
     scale, fp_in, w1_in, w2_in, o1, o2,
     fp, fpt, w1, w2, hid, hidt, emb, summed, gate, demb, dpre, sqc, sqr,
-    xo1, xo2, xb1, xb2, zs1, zs2, zb1, zb2, ys1, ys2, yb1, yb2,
-    load_sem, send_sem, recv_sem, pass_send, pass_recv, xs, xr, zs, zr, ys, yr,
+    gx, rx, gy, ry, gz, rz, hx, qx, hy, qy, hz, qz, kxy, rxy, kz, r3z, f1, r1, f2, r2,
+    load_sem, send_sem, recv_sem, pass_send, pass_recv,
+    xs, xr, ys, yr, zs, zr, xs2, xr2, ys2, yr2, zs2, zr2, s3, t3, zs3, zr3, s4, t4,
 ):
     blk = lax.axis_index("blk")
     dp = lax.axis_index("dp")
@@ -44,15 +45,17 @@
     def at(z, x, y, c):
         return {"blk": (y // 2) * 2 + c, "dp": (z * NX + x) * 2 + y % 2}
 
+    side = y % 2
     far = at(z, x, (y + 2) % 4, c)
     near = at(z, x, y, 1 - c)
+    cross_far = at(z, x, (y + 2) % 4, 1 - c)
+    pair = at(z, x, (y // 2) * 2 + 1 - side, c)
     x_peers = [at(z, (x + k) % NX, y, c) for k in range(1, NX)]
     z_peers = [at((z + k) % NZ, x, y, c) for k in range(1, NZ)]
-    y_steps = [(dy, dc) for dy in range(4) for dc in range(2)][1:]
-    y_peers = [at(z, x, (y + dy) % 4, (c + dc) % 2) for dy, dc in y_steps]
+    peers = [far, near, cross_far, pair] + x_peers + z_peers
 
     barrier = pltpu.get_barrier_semaphore()
-    for peer in y_peers + x_peers + z_peers:
+    for peer in peers:
         pl.semaphore_signal(barrier, inc=1, device_id=peer, device_id_type=MESH)
     loads = [
         pltpu.make_async_copy(fp_in, fp.at[pl.ds(0, tok)], load_sem.at[0]),
@@ -61,7 +64,7 @@
     ]
     for load in loads:
         load.start()
-    pl.semaphore_wait(barrier, len(x_peers) + len(z_peers) + len(y_peers))
+    pl.semaphore_wait(barrier, len(peers))
 
     def remote(src, dst, send, recv, peer):
         return pltpu.make_async_remote_copy(
@@ -161,93 +164,123 @@
             cross(pl.ds(pl.multiple_of(half + i * T, T), T), rows)
 
     demb[...] = (summed[...] * scale).astype(BF16)
+    cols = width // 4
+    part = dot_nn(hidt[...], demb[:, pl.ds(pl.multiple_of(blk * cols, cols), cols)])
+    gz[...] = part.astype(BF16).reshape(gz.shape)
+    z_copies = [
+        remote(gz.at[(z + k) % NZ], rz.at[k - 1], zs.at[k - 1], zr.at[k - 1], z_peers[k - 1])
+        for k in (4, 3, 5, 2, 6, 1, 7)
+    ]
+    for copy in z_copies:
+        copy.start()
+
     quarter = pl.ds(pl.multiple_of(blk * T, T), T)
     for r in range(0, rows_all, 2 * T):
         rows = pl.ds(r, 2 * T)
         back = dot_nt(demb[rows, :], w2[quarter, :])
         dpre[rows, :] = (back * gate[rows, quarter]).astype(BF16)
 
-    def scatter_x(part, out, z0, step):
-        sub = step // NX
-        for k in range(part.shape[0] // step):
+    x_copies, y_copies = [], []
+    span = NZ // 2
+    own = gy.shape[3]
+    for i in range(2):
+        rows = pl.ds(i * d_in // 2, d_in // 2)
+        part = dot_nn(fpt[rows, :], dpre[...]).astype(BF16)
+        for k in range(span):
+            zz = i * span + k
             for xx in range(NX):
-                out[xx, pl.ds((z0 + k) * sub, sub), :] = part[
-                    k * step + xx * sub : k * step + (xx + 1) * sub
-                ].astype(BF16)
-
-    def send_x(src, dst, sems):
+                for ll in range(2):
+                    line = ((k * NX + xx) * 2 + ll) * own
+                    gx[xx, zz, ll * own : (ll + 1) * own, :] = part[line : line + own, :128]
+                    gy[ll, zz, xx] = part[line : line + own, 128:]
+        zz = pl.ds(i * span, span)
+        copy = remote(gy.at[1 - side, zz], ry.at[zz], ys.at[i], yr.at[i], pair)
+        y_copies.append(copy)
+        copy.start()
         for k in (2, 1, 3):
-            to = (x + k) % NX
             copy = remote(
-                src(to), dst(k - 1), xs.at[sems, k - 1], xr.at[sems, k - 1], x_peers[k - 1]
+                gx.at[(x + k) % NX, zz], rx.at[k - 1, zz],
+                xs.at[i, k - 1], xr.at[i, k - 1], x_peers[k - 1],
             )
-            copies.append(copy)
+            x_copies.append(copy)
             copy.start()
 
-    copies = []
-    for part in range(2):
-        span = d_in // 2
-        scatter_x(
-            dot_nn(fpt[pl.ds(part * span, span), :], dpre[...]),
-            xo1, part * NZ // 2, d_in // NZ,
-        )
-        lines = pl.ds(part * span // NX, span // NX)
-        send_x(lambda to: xo1.at[to, lines], lambda k: xb1.at[k, lines], part)
-    cols = width // 4
-    scatter_x(
-        dot_nn(hidt[...], demb[:, pl.ds(pl.multiple_of(blk * cols, cols), cols)]),
-        xo2, 0, hidden // NZ,
-    )
-    send_x(lambda to: xo2.at[to], lambda k: xb2.at[k], 2)
+    def total(mine, others):
+        out = mine.astype(F32)
+        for k in range(others.shape[0]):
+            out = out + others[k].astype(F32)
+        return out
+
+    for copy in y_copies:
+        copy.wait()
+    for xx in range(NX):
+        hy[xx] = (gy[side, :, xx].astype(F32) + ry[:, xx].astype(F32)).astype(BF16)
+    y_copies = [
+        remote(hy.at[(x + k) % NX], qy.at[k - 1], ys2.at[k - 1], yr2.at[k - 1], x_peers[k - 1])
+        for k in (2, 1, 3)
+    ]
+    for copy in y_copies:
+        copy.start()
+
+    for copy in x_copies:
+        copy.wait()
+    part = total(gx[x], rx).astype(BF16)
+    for ll in range(2):
+        hx[ll] = part[:, ll * own : (ll + 1) * own, :]
+    x_copy = remote(hx.at[1 - side], qx, xs2, xr2, pair)
+    x_copy.start()
+
+    for copy in z_copies:
+        copy.wait()
+    hz[...] = total(gz[z], rz).astype(BF16).reshape(hz.shape)
+    z_copies = [
+        remote(hz.at[(x + k) % NX], qz.at[k - 1], zs2.at[k - 1], zr2.at[k - 1], x_peers[k - 1])
+        for k in (2, 1, 3)
+    ]
+    for copy in z_copies:
+        copy.start()
+
+    x_copy.wait()
+    kxy[:, :, :128] = (hx[side].astype(F32) + qx[...].astype(F32)).astype(BF16)
+    for copy in y_copies:
+        copy.wait()
+    kxy[:, :, 128:] = total(hy[x], qy).astype(BF16)
+    copies = [
+        remote(kxy.at[(z + k) % NZ], rxy.at[k - 1], s3.at[k - 1], t3.at[k - 1], z_peers[k - 1])
+        for k in (4, 3, 5, 2, 6, 1, 7)
+    ]
     for copy in copies:
-        copy.wait()
-
-    def sum_x(own, buf):
-        total = own[x].astype(F32)
-        for k in range(NX - 1):
-            total = total + buf[k].astype(F32)
-        return total
-
-    zs1[...] = sum_x(xo1, xb1).astype(BF16).reshape(zs1.shape)
-    zs2[...] = sum_x(xo2, xb2).astype(BF16).reshape(zs2.shape)
-
-    copies = []
-    for k in (4, 3, 5, 2, 6, 1, 7):
-        peer, to = z_peers[k - 1], (z + k) % NZ
-        copies.append(remote(zs1.at[to], zb1.at[k - 1], zs.at[0, k - 1], zr.at[0, k - 1], peer))
-        copies.append(remote(zs2.at[to], zb2.at[k - 1], zs.at[1, k - 1], zr.at[1, k - 1], peer))
+        copy.start()
+
+    for copy in z_copies:
+        copy.wait()
+    kz[...] = total(hz[x], qz).reshape(kz.shape)
+    z_copy = remote(kz.at[1 - side], r3z, zs3, zr3, pair)
+    z_copy.start()
+    z_copy.wait()
+    f2[...] = kz[side] + r3z[...]
+
+    def spread(src, dst, i):
+        out = [
+            remote(src, dst.at[blk], s4.at[i, k], t4.at[i, k], peer)
+            for k, peer in enumerate((cross_far, far, near))
+        ]
+        for copy in out:
+            copy.start()
+        return out
+
+    last = spread(f2, r2, 0)
     for copy in copies:
-        copy.start()
-    for copy in copies:
-        copy.wait()
-
-    def sum_z(own, buf):
-        total = own[z].astype(F32)
-        for k in range(NZ - 1):
-            total = total + buf[k].astype(F32)
-        return total
-
-    ys1[...] = sum_z(zs1, zb1).reshape(ys1.shape)
-    ys2[...] = sum_z(zs2, zb2).reshape(ys2.shape)
-
-    copies = []
-    for k, (dy, dc) in enumerate(y_steps):
-        peer, to = y_peers[k], (y + dy) % 2
-        slot = y * 2 + c
-        copies.append(remote(ys1.at[to], yb1.at[slot], ys.at[0, k], yr.at[0, k], peer))
-        copies.append(remote(ys2.at[to], yb2.at[slot], ys.at[1, k], yr.at[1, k], peer))
-    for copy in copies:
-        copy.start()
-    yb1[y * 2 + c] = ys1[y % 2]
-    yb2[y * 2 + c] = ys2[y % 2]
-    for copy in copies:
-        copy.wait()
-    for h in range(2):
-        for core in range(2):
-            q = 2 * h + core
-            low, high = 4 * h + core, 4 * h + 2 + core
-            o1[:, q * o1.shape[1] // 4 : (q + 1) * o1.shape[1] // 4] = yb1[low] + yb1[high]
-            o2[:, q * o2.shape[1] // 4 : (q + 1) * o2.shape[1] // 4] = yb2[low] + yb2[high]
+        copy.wait()
+    f1[...] = total(kxy[z], rxy)
+    last += spread(f1, r1, 1)
+    r1[blk] = f1[...]
+    r2[blk] = f2[...]
+    for copy in last:
+        copy.wait()
+    for q in range(4):
+        o1[:, q * o1.shape[1] // 4 : (q + 1) * o1.shape[1] // 4] = r1[q]
+        o2[:, q * o2.shape[1] // 4 : (q + 1) * o2.shape[1] // 4] = r2[q]
 
 
 def gradients(fingerprints, w_first, w_second, scale):
@@ -257,15 +290,14 @@
     pieces = tok // HALF
     any_spec = pl.BlockSpec(memory_space=pl.ANY)
     vmem_spec = pl.BlockSpec(memory_space=pltpu.VMEM)
-    r1, c1 = d_in // NX, hidden // 4
-    r2, c2 = hidden // NX, width // 4
-    z1, z2 = r1 // NZ, r2 // NZ
+    c1, c2 = hidden // 4, width // 4
+    n1, n2 = d_in // (NZ * NX * 2), hidden // (NZ * NX * 2)
     dma = pltpu.SemaphoreType.DMA
     return pl.pallas_call(
         functools.partial(step_kernel, scale),
         out_shape=(
-            jax.ShapeDtypeStruct((z1 // 2, 4 * c1), F32),
-            jax.ShapeDtypeStruct((z2 // 2, 4 * c2), F32),
+            jax.ShapeDtypeStruct((n1, 4 * c1), F32),
+            jax.ShapeDtypeStruct((n2, 4 * c2), F32),
         ),
         in_specs=[any_spec] * 3,
         out_specs=(vmem_spec, vmem_spec),
@@ -283,29 +315,49 @@
             pltpu.VMEM((rows, hidden // 4), BF16),
             pltpu.VMEM((rows, 128), F32),
             pltpu.VMEM((8, rows), F32),
-            pltpu.VMEM((NX, r1, c1), BF16),
-            pltpu.VMEM((NX, r2, c2), BF16),
-            pltpu.VMEM((NX - 1, r1, c1), BF16),
-            pltpu.VMEM((NX - 1, r2, c2), BF16),
-            pltpu.VMEM((NZ, z1, c1), BF16),
-            pltpu.VMEM((NZ, z2, c2), BF16),
-            pltpu.VMEM((NZ - 1, z1, c1), BF16),
-            pltpu.VMEM((NZ - 1, z2, c2), BF16),
-            pltpu.VMEM((2, z1 // 2, c1), F32),
-            pltpu.VMEM((2, z2 // 2, c2), F32),
-            pltpu.VMEM((8, z1 // 2, c1), F32),
-            pltpu.VMEM((8, z2 // 2, c2), F32),
+            pltpu.VMEM((NX, NZ, 2 * n1, 128), BF16),
+            pltpu.VMEM((NX - 1, NZ, 2 * n1, 128), BF16),
+            pltpu.VMEM((2, NZ, NX, n1, 128), BF16),
+            pltpu.VMEM((NZ, NX, n1, 128), BF16),
+            pltpu.VMEM((NZ, NX * 2 * n2, c2), BF16),
+            pltpu.VMEM((NZ - 1, NX * 2 * n2, c2), BF16),
+            pltpu.VMEM((2, NZ, n1, 128), BF16),
+            pltpu.VMEM((NZ, n1, 128), BF16),
+            pltpu.VMEM((NX, NZ, n1, 128), BF16),
+            pltpu.VMEM((NX - 1, NZ, n1, 128), BF16),
+            pltpu.VMEM((NX, 2 * n2, c2), BF16),
+            pltpu.VMEM((NX - 1, 2 * n2, c2), BF16),
+            pltpu.VMEM((NZ, n1, c1), BF16),
+            pltpu.VMEM((NZ - 1, n1, c1), BF16),
+            pltpu.VMEM((2, n2, c2), F32),
+            pltpu.VMEM((n2, c2), F32),
+            pltpu.VMEM((n1, c1), F32),
+            pltpu.VMEM((4, n1, c1), F32),
+            pltpu.VMEM((n2, c2), F32),
+            pltpu.VMEM((4, n2, c2), F32),
             dma((3,)),
             dma((pieces + 1,)),
             dma((pieces + 1,)),
             dma((pieces,)),
             dma((pieces,)),
-            dma((3, NX - 1)),
-            dma((3, NX - 1)),
-            dma((2, NZ - 1)),
-            dma((2, NZ - 1)),
-            dma((2, 7)),
-            dma((2, 7)),
+            dma((2, NX - 1)),
+            dma((2, NX - 1)),
+            dma((2,)),
+            dma((2,)),
+            dma((NZ - 1,)),
+            dma((NZ - 1,)),
+            dma,
+            dma,
+            dma((NX - 1,)),
+            dma((NX - 1,)),
+            dma((NX - 1,)),
+            dma((NX - 1,)),
+            dma((NZ - 1,)),
+            dma((NZ - 1,)),
+            dma,
+            dma,
+            dma((2, 3)),
+            dma((2, 3)),
         ],
         compiler_params=pltpu.CompilerParams(
             collective_id=0, has_side_effects=True, vmem_limit_bytes=60 << 20

time: 93.8 us -> 86.6 us (0.923)
  Pallas kernels: 90 us -> 82.8 us
    pallas_call x1, Pallas kernels: 90 us -> 82.8 us  [gradients(): pl.pallas_call(functools.partial(step_kernel, scale), out_shape=(jax.Shap...]
where the time goes in v3:
time: 86.6 us; the launch traced here: 86.4 us
  Pallas kernels  82.8 us (96%)
  local copies, waits for them, and re-layouts  2.94 us (3%)
    pallas_call x1, Pallas kernels, gradients(): pl.pallas_call(functools.partial(step_kernel, scale), out_shape=(jax.Shap...  82.8 us
    unnamed x2, local copies, waits for them, and re-layouts  2.94 us

profile of v3, /device:TPU:1, one launch (start us, length us, event | category | flops | bytes accessed | tf_op | source)
XLA Modules:
  0.0 86.4 jit_solution(5435945947609151490)
XLA Ops:
  0.6 82.8 %gradients.1 = (f32[32,1024]{1,0:T(8,128)}, f32[16,512]{1,0:T(8,128)}) custom-call(bf16[384,2048]{1,0:T(8,128)(2,1)} %fp_in.1, bf16[2048,1024]{1,0:T(8,128)(2,1)} %w1_in.1, bf16[1024,512]{1,0:T(8,128)(2,1)} %w2_in.1), custom_call_target="tpu_custom_call" | custom-call | tf_op jit(solution)/shard_map/gradients/pallas_call | solution.py:296
  83.5 1.6 %copy.7 = f32[32,1024]{1,0:T(8,128)} copy(f32[32,1024]{1,0:T(8,128)} %get-tuple-element.4) | data formatting | bytes 262144
  85.0 1.4 %copy.8 = f32[16,512]{1,0:T(8,128)} copy(f32[16,512]{1,0:T(8,128)} %get-tuple-element.5) | data formatting | bytes 65536

commit v4 on v3

--- a/solution.py
+++ b/solution.py
@@ -27,9 +27,9 @@
 def step_kernel(
     scale, fp_in, w1_in, w2_in, o1, o2,
     fp, fpt, w1, w2, hid, hidt, emb, summed, gate, demb, dpre, sqc, sqr,
-    gx, rx, gy, ry, gz, rz, hx, qx, hy, qy, hz, qz, kxy, rxy, kz, r3z, f1, r1, f2, r2,
+    gx, rx, gy, ry, gz, rz, hx, qx, hy, qy, hz, qz, kx, r3x, ky, qky, kz, r3z, f1, r1, f2, r2,
     load_sem, send_sem, recv_sem, pass_send, pass_recv,
-    xs, xr, ys, yr, zs, zr, xs2, xr2, ys2, yr2, zs2, zr2, s3, t3, zs3, zr3, s4, t4,
+    xs, xr, ys, yr, zs, zr, xs2, xr2, ys2, yr2, zs2, zr2, xs3, xr3, s3, t3, zs3, zr3, s4, t4,
 ):
     blk = lax.axis_index("blk")
     dp = lax.axis_index("dp")
@@ -224,15 +224,17 @@
 
     for copy in x_copies:
         copy.wait()
-    part = total(gx[x], rx).astype(BF16)
-    for ll in range(2):
-        hx[ll] = part[:, ll * own : (ll + 1) * own, :]
-    x_copy = remote(hx.at[1 - side], qx, xs2, xr2, pair)
-    x_copy.start()
+    hx[...] = total(gx[x], rx).astype(BF16)
+    x_copies = [
+        remote(hx.at[(z + k) % NZ], qx.at[k - 1], xs2.at[k - 1], xr2.at[k - 1], z_peers[k - 1])
+        for k in (4, 3, 5, 2, 6, 1, 7)
+    ]
+    for copy in x_copies:
+        copy.start()
 
     for copy in z_copies:
         copy.wait()
-    hz[...] = total(gz[z], rz).astype(BF16).reshape(hz.shape)
+    hz[...] = total(gz[z], rz).reshape(hz.shape)
     z_copies = [
         remote(hz.at[(x + k) % NX], qz.at[k - 1], zs2.at[k - 1], zr2.at[k - 1], x_peers[k - 1])
         for k in (2, 1, 3)
@@ -240,13 +242,11 @@
     for copy in z_copies:
         copy.start()
 
-    x_copy.wait()
-    kxy[:, :, :128] = (hx[side].astype(F32) + qx[...].astype(F32)).astype(BF16)
     for copy in y_copies:
         copy.wait()
-    kxy[:, :, 128:] = total(hy[x], qy).astype(BF16)
+    ky[...] = total(hy[x], qy)
     copies = [
-        remote(kxy.at[(z + k) % NZ], rxy.at[k - 1], s3.at[k - 1], t3.at[k - 1], z_peers[k - 1])
+        remote(ky.at[(z + k) % NZ], qky.at[k - 1], s3.at[k - 1], t3.at[k - 1], z_peers[k - 1])
         for k in (4, 3, 5, 2, 6, 1, 7)
     ]
     for copy in copies:
@@ -257,6 +257,11 @@
     kz[...] = total(hz[x], qz).reshape(kz.shape)
     z_copy = remote(kz.at[1 - side], r3z, zs3, zr3, pair)
     z_copy.start()
+    for copy in x_copies:
+        copy.wait()
+    kx[...] = total(hx[z], qx).reshape(kx.shape)
+    x_copy = remote(kx.at[1 - side], r3x, xs3, xr3, pair)
+    x_copy.start()
     z_copy.wait()
     f2[...] = kz[side] + r3z[...]
 
@@ -270,9 +275,11 @@
         return out
 
     last = spread(f2, r2, 0)
+    x_copy.wait()
+    f1[:, :128] = kx[side] + r3x[...]
     for copy in copies:
         copy.wait()
-    f1[...] = total(kxy[z], rxy)
+    f1[:, 128:] = total(ky[z], qky)
     last += spread(f1, r1, 1)
     r1[blk] = f1[...]
     r2[blk] = f2[...]
@@ -321,14 +328,16 @@
             pltpu.VMEM((NZ, NX, n1, 128), BF16),
             pltpu.VMEM((NZ, NX * 2 * n2, c2), BF16),
             pltpu.VMEM((NZ - 1, NX * 2 * n2, c2), BF16),
-            pltpu.VMEM((2, NZ, n1, 128), BF16),
-            pltpu.VMEM((NZ, n1, 128), BF16),
+            pltpu.VMEM((NZ, 2 * n1, 128), BF16),
+            pltpu.VMEM((NZ - 1, 2 * n1, 128), BF16),
             pltpu.VMEM((NX, NZ, n1, 128), BF16),
             pltpu.VMEM((NX - 1, NZ, n1, 128), BF16),
-            pltpu.VMEM((NX, 2 * n2, c2), BF16),
-            pltpu.VMEM((NX - 1, 2 * n2, c2), BF16),
-            pltpu.VMEM((NZ, n1, c1), BF16),
-            pltpu.VMEM((NZ - 1, n1, c1), BF16),
+            pltpu.VMEM((NX, 2 * n2, c2), F32),
+            pltpu.VMEM((NX - 1, 2 * n2, c2), F32),
+            pltpu.VMEM((2, n1, 128), F32),
+            pltpu.VMEM((n1, 128), F32),
+            pltpu.VMEM((NZ, n1, 128), F32),
+            pltpu.VMEM((NZ - 1, n1, 128), F32),
             pltpu.VMEM((2, n2, c2), F32),
             pltpu.VMEM((n2, c2), F32),
             pltpu.VMEM((n1, c1), F32),
@@ -346,12 +355,14 @@
             dma((2,)),
             dma((NZ - 1,)),
             dma((NZ - 1,)),
-            dma,
-            dma,
+            dma((NZ - 1,)),
+            dma((NZ - 1,)),
             dma((NX - 1,)),
             dma((NX - 1,)),
             dma((NX - 1,)),
             dma((NX - 1,)),
+            dma,
+            dma,
             dma((NZ - 1,)),
             dma((NZ - 1,)),
             dma,

time: 86.6 us -> 86.7 us (level)
  no operation moved by 1% of the time
where the time goes in v4:
time: 86.7 us; the launch traced here: 86.5 us
  Pallas kernels  83 us (96%)
  local copies, waits for them, and re-layouts  2.94 us (3%)
    pallas_call x1, Pallas kernels, gradients(): pl.pallas_call(functools.partial(step_kernel, scale), out_shape=(jax.Shap...  83 us
    unnamed x2, local copies, waits for them, and re-layouts  2.94 us

profile of v4, /device:TPU:1, one launch (start us, length us, event | category | flops | bytes accessed | tf_op | source)
XLA Modules:
  0.0 86.5 jit_solution(4558273622513674896)
XLA Ops:
  0.6 83.0 %gradients.1 = (f32[32,1024]{1,0:T(8,128)}, f32[16,512]{1,0:T(8,128)}) custom-call(bf16[384,2048]{1,0:T(8,128)(2,1)} %fp_in.1, bf16[2048,1024]{1,0:T(8,128)(2,1)} %w1_in.1, bf16[1024,512]{1,0:T(8,128)(2,1)} %w2_in.1), custom_call_target="tpu_custom_call" | custom-call | tf_op jit(solution)/shard_map/gradients/pallas_call | solution.py:303
  83.6 1.6 %copy.7 = f32[32,1024]{1,0:T(8,128)} copy(f32[32,1024]{1,0:T(8,128)} %get-tuple-element.4) | data formatting | bytes 262144
  85.2 1.4 %copy.8 = f32[16,512]{1,0:T(8,128)} copy(f32[16,512]{1,0:T(8,128)} %get-tuple-element.5) | data formatting | bytes 65536

commit v5 on v4

--- a/solution.py
+++ b/solution.py
@@ -13,7 +13,7 @@
 BF16 = jnp.bfloat16
 NZ, NX = 8, 4
 T = 256
-HALF = 128
+SPLIT = (3, 2, 1)
 
 
 def dot_nt(a, b):
@@ -39,7 +39,9 @@
     hidden, width = w2_in.shape
     half = 2 * tok
     rows_all = 4 * tok
-    pieces = tok // HALF
+    pieces = len(SPLIT)
+    sizes = [tok * share // sum(SPLIT) for share in SPLIT]
+    firsts = [sum(sizes[:p]) for p in range(pieces)]
     norm = 1.0 / math.sqrt(width)
 
     def at(z, x, y, c):
@@ -74,13 +76,15 @@
 
     def far_copy(p):
         return remote(
-            fp_in.at[pl.ds(p * HALF, HALF)], fp.at[pl.ds(half + p * T, HALF)],
+            fp_in.at[pl.ds(firsts[p], sizes[p])],
+            fp.at[pl.ds(half + 2 * firsts[p], sizes[p])],
             send_sem.at[p], recv_sem.at[p], far,
         )
 
     def passing(p):
         return remote(
-            fp.at[pl.ds(half + p * T, HALF)], fp.at[pl.ds(half + p * T + HALF, HALF)],
+            fp.at[pl.ds(half + 2 * firsts[p], sizes[p])],
+            fp.at[pl.ds(half + 2 * firsts[p] + sizes[p], sizes[p])],
             pass_send.at[p], pass_recv.at[p], near,
         )
 
@@ -111,18 +115,19 @@
         pred = dot_nt(emb[upper, :], emb[lower, :])
         return (pred * norm - inter / den).astype(BF16)
 
-    def diagonal(rows):
+    def diagonal(first, count):
+        rows = pl.ds(first, count)
         inter = dot_nt(fp[rows, :], fp[rows, :])
-        r_id = lax.broadcasted_iota(jnp.int32, (T, T), 0)
-        c_id = lax.broadcasted_iota(jnp.int32, (T, T), 1)
+        r_id = lax.broadcasted_iota(jnp.int32, (count, count), 0)
+        c_id = lax.broadcasted_iota(jnp.int32, (count, count), 1)
         diag = jnp.where(r_id == c_id, inter, 0.0)
         col = jnp.sum(diag, axis=1, keepdims=True)
         row = jnp.sum(diag, axis=0, keepdims=True)
-        sqc[rows, :] = jnp.broadcast_to(col, (T, 128))
-        sqr[:, rows] = jnp.broadcast_to(row, (8, T))
+        sqc[rows, :] = jnp.broadcast_to(col, (count, 128))
+        sqr[:, rows] = jnp.broadcast_to(row, (8, count))
         pred = dot_nt(emb[rows, :], emb[rows, :])
         resid = (pred * norm - inter / (col + row - inter)).astype(BF16)
-        return dot_nn(resid, emb[rows, :])
+        summed[rows, :] = dot_nn(resid, emb[rows, :])
 
     def cross(upper, lower):
         resid = residual(upper, lower)
@@ -141,13 +146,13 @@
 
     embed(pl.ds(0, half), half)
     for r in range(0, half, T):
-        summed[pl.ds(r, T), :] = diagonal(pl.ds(r, T))
+        diagonal(r, T)
         if r:
             cross(pl.ds(0, r), pl.ds(r, T))
 
-    @pl.loop(0, pieces)
-    def _(p):
-        rows = pl.ds(pl.multiple_of(half + p * T, T), T)
+    for p in range(pieces):
+        first, count = half + 2 * firsts[p], 2 * sizes[p]
+        rows = pl.ds(first, count)
         far_copy(p).wait()
         passing(p).start()
         passing(p).wait()
@@ -155,25 +160,13 @@
             encode_columns(rows, pl.ds(n, T))
         for n in range(0, d_in, T):
             fpt[pl.ds(n, T), rows] = fp[rows, pl.ds(n, T)].T
-        embed(rows, T)
-        summed[rows, :] = diagonal(rows)
+        embed(rows, count)
+        diagonal(first, count)
         cross(pl.ds(0, half), rows)
-
-        @pl.loop(0, p)
-        def _(i):
-            cross(pl.ds(pl.multiple_of(half + i * T, T), T), rows)
+        if p:
+            cross(pl.ds(half, first - half), rows)
 
     demb[...] = (summed[...] * scale).astype(BF16)
-    cols = width // 4
-    part = dot_nn(hidt[...], demb[:, pl.ds(pl.multiple_of(blk * cols, cols), cols)])
-    gz[...] = part.astype(BF16).reshape(gz.shape)
-    z_copies = [
-        remote(gz.at[(z + k) % NZ], rz.at[k - 1], zs.at[k - 1], zr.at[k - 1], z_peers[k - 1])
-        for k in (4, 3, 5, 2, 6, 1, 7)
-    ]
-    for copy in z_copies:
-        copy.start()
-
     quarter = pl.ds(pl.multiple_of(blk * T, T), T)
     for r in range(0, rows_all, 2 * T):
         rows = pl.ds(r, 2 * T)
@@ -205,22 +198,36 @@
             x_copies.append(copy)
             copy.start()
 
+    cols = width // 4
+    part = dot_nn(hidt[...], demb[:, pl.ds(pl.multiple_of(blk * cols, cols), cols)])
+    gz[...] = part.astype(BF16).reshape(gz.shape)
+    z_copies = [
+        remote(gz.at[(z + k) % NZ], rz.at[k - 1], zs.at[k - 1], zr.at[k - 1], z_peers[k - 1])
+        for k in (4, 3, 5, 2, 6, 1, 7)
+    ]
+    for copy in z_copies:
+        copy.start()
+
     def total(mine, others):
         out = mine.astype(F32)
         for k in range(others.shape[0]):
             out = out + others[k].astype(F32)
         return out
 
-    for copy in y_copies:
-        copy.wait()
-    for xx in range(NX):
-        hy[xx] = (gy[side, :, xx].astype(F32) + ry[:, xx].astype(F32)).astype(BF16)
-    y_copies = [
-        remote(hy.at[(x + k) % NX], qy.at[k - 1], ys2.at[k - 1], yr2.at[k - 1], x_peers[k - 1])
-        for k in (2, 1, 3)
-    ]
-    for copy in y_copies:
-        copy.start()
+    more = []
+    for i in range(2):
+        y_copies[i].wait()
+        zz = pl.ds(i * span, span)
+        for xx in range(NX):
+            hy[xx, zz] = (gy[side, zz, xx].astype(F32) + ry[zz, xx].astype(F32)).astype(BF16)
+        for k in (2, 1, 3):
+            copy = remote(
+                hy.at[(x + k) % NX, zz], qy.at[k - 1, zz],
+                ys2.at[i, k - 1], yr2.at[i, k - 1], x_peers[k - 1],
+            )
+            more.append(copy)
+            copy.start()
+    y_copies = more
 
     for copy in x_copies:
         copy.wait()
@@ -276,17 +283,20 @@
 
     last = spread(f2, r2, 0)
     x_copy.wait()
-    f1[:, :128] = kx[side] + r3x[...]
+    f1[0] = kx[side] + r3x[...]
+    last += spread(f1.at[0], r1.at[0], 1)
     for copy in copies:
         copy.wait()
-    f1[:, 128:] = total(ky[z], qky)
-    last += spread(f1, r1, 1)
-    r1[blk] = f1[...]
+    f1[1] = total(ky[z], qky)
+    last += spread(f1.at[1], r1.at[1], 2)
+    for i in range(2):
+        r1[i, blk] = f1[i]
     r2[blk] = f2[...]
     for copy in last:
         copy.wait()
     for q in range(4):
-        o1[:, q * o1.shape[1] // 4 : (q + 1) * o1.shape[1] // 4] = r1[q]
+        for i in range(2):
+            o1[:, (2 * q + i) * 128 : (2 * q + i + 1) * 128] = r1[i, q]
         o2[:, q * o2.shape[1] // 4 : (q + 1) * o2.shape[1] // 4] = r2[q]
 
 
@@ -294,8 +304,8 @@
     tok, d_in = fingerprints.shape
     hidden, width = w_second.shape
     rows = 4 * tok
-    pieces = tok // HALF
-    any_spec = pl.BlockSpec(memory_space=pl.ANY)
+    pieces = len(SPLIT)
+    hbm_spec = pl.BlockSpec(memory_space=pltpu.HBM)
     vmem_spec = pl.BlockSpec(memory_space=pltpu.VMEM)
     c1, c2 = hidden // 4, width // 4
     n1, n2 = d_in // (NZ * NX * 2), hidden // (NZ * NX * 2)
@@ -306,7 +316,7 @@
             jax.ShapeDtypeStruct((n1, 4 * c1), F32),
             jax.ShapeDtypeStruct((n2, 4 * c2), F32),
         ),
-        in_specs=[any_spec] * 3,
+        in_specs=[hbm_spec] * 3,
         out_specs=(vmem_spec, vmem_spec),
         scratch_shapes=[
             pltpu.VMEM((rows, d_in), BF16),
@@ -340,8 +350,8 @@
             pltpu.VMEM((NZ - 1, n1, 128), F32),
             pltpu.VMEM((2, n2, c2), F32),
             pltpu.VMEM((n2, c2), F32),
-            pltpu.VMEM((n1, c1), F32),
-            pltpu.VMEM((4, n1, c1), F32),
+            pltpu.VMEM((2, n1, 128), F32),
+            pltpu.VMEM((2, 4, n1, 128), F32),
             pltpu.VMEM((n2, c2), F32),
             pltpu.VMEM((4, n2, c2), F32),
             dma((3,)),
@@ -357,8 +367,8 @@
             dma((NZ - 1,)),
             dma((NZ - 1,)),
             dma((NZ - 1,)),
-            dma((NX - 1,)),
-            dma((NX - 1,)),
+            dma((2, NX - 1)),
+            dma((2, NX - 1)),
             dma((NX - 1,)),
             dma((NX - 1,)),
             dma,
@@ -367,11 +377,11 @@
             dma((NZ - 1,)),
             dma,
             dma,
-            dma((2, 3)),
-            dma((2, 3)),
+            dma((3, 3)),
+            dma((3, 3)),
         ],
         compiler_params=pltpu.CompilerParams(
-            collective_id=0, has_side_effects=True, vmem_limit_bytes=60 << 20
+            collective_id=0, has_side_effects=True, vmem_limit_bytes=55500000
         ),
         name="gradients",
     )(fingerprints, w_first, w_second)

time: 86.7 us -> 82.9 us (0.956)
  Pallas kernels: 83 us -> 80.9 us
  local copies, waits for them, and re-layouts: 2.94 us -> 1.27 us
    pallas_call x1, Pallas kernels: 83 us -> 80.9 us  [gradients(): pl.pallas_call(functools.partial(step_kernel, scale), out_shape=(jax.Shap...]
    unnamed x2, local copies, waits for them, and re-layouts: 2.94 us -> 1.27 us
where the time goes in v5:
time: 82.9 us; the launch traced here: 82.8 us
  Pallas kernels  80.9 us (98%)
  local copies, waits for them, and re-layouts  1.27 us (2%)
    pallas_call x1, Pallas kernels, gradients(): pl.pallas_call(functools.partial(step_kernel, scale), out_shape=(jax.Shap...  80.9 us

profile of v5, /device:TPU:1, one launch (start us, length us, event | category | flops | bytes accessed | tf_op | source)
XLA Modules:
  0.0 82.8 jit_solution(13685536355050521713)
XLA Ops:
  0.6 80.9 %gradients.1 = (f32[32,1024]{1,0:T(8,128)S(1)}, f32[16,512]{1,0:T(8,128)S(1)}) custom-call(bf16[384,2048]{1,0:T(8,128)(2,1)} %fp_in.1, bf16[2048,1024]{1,0:T(8,128)(2,1)} %w1_in.1, bf16[1024,512]{1,0:T(8,128)(2,1)} %w2_in.1), custom_call_target="tpu_custom_call" | custom-call | tf_op jit(solution)/shard_map/gradients/pallas_call | solution.py:313
  81.5 0.7 copy.7
  82.2 0.6 copy.8

commit v6 on v5

--- a/solution.py
+++ b/solution.py
@@ -13,7 +13,8 @@
 BF16 = jnp.bfloat16
 NZ, NX = 8, 4
 T = 256
-SPLIT = (3, 2, 1)
+PARTS = 4
+SPLIT = (2, 2, 1, 1)
 
 
 def dot_nt(a, b):
@@ -28,7 +29,7 @@
     scale, fp_in, w1_in, w2_in, o1, o2,
     fp, fpt, w1, w2, hid, hidt, emb, summed, gate, demb, dpre, sqc, sqr,
     gx, rx, gy, ry, gz, rz, hx, qx, hy, qy, hz, qz, kx, r3x, ky, qky, kz, r3z, f1, r1, f2, r2,
-    load_sem, send_sem, recv_sem, pass_send, pass_recv,
+    ready, load_sem, send_sem, recv_sem, pass_send, pass_recv,
     xs, xr, ys, yr, zs, zr, xs2, xr2, ys2, yr2, zs2, zr2, xs3, xr3, s3, t3, zs3, zr3, s4, t4,
 ):
     blk = lax.axis_index("blk")
@@ -54,7 +55,8 @@
     pair = at(z, x, (y // 2) * 2 + 1 - side, c)
     x_peers = [at(z, (x + k) % NX, y, c) for k in range(1, NX)]
     z_peers = [at((z + k) % NZ, x, y, c) for k in range(1, NZ)]
-    peers = [far, near, cross_far, pair] + x_peers + z_peers
+    steps = [z_peers[k % NZ - 1] for k in (2, -2)]
+    peers = [far, near, cross_far, pair] + x_peers + steps + [z_peers[0], z_peers[NZ - 2]]
 
     barrier = pltpu.get_barrier_semaphore()
     for peer in peers:
@@ -64,8 +66,7 @@
         pltpu.make_async_copy(w1_in, w1, load_sem.at[1]),
         pltpu.make_async_copy(w2_in, w2, load_sem.at[2]),
     ]
-    for load in loads:
-        load.start()
+    loads[0].start()
     pl.semaphore_wait(barrier, len(peers))
 
     def remote(src, dst, send, recv, peer):
@@ -94,6 +95,10 @@
     for p in range(pieces):
         far_copy(p).start()
     near_copy.start()
+    for load in loads[1:]:
+        load.start()
+    for peer in steps:
+        pl.semaphore_signal(ready, inc=1, device_id=peer, device_id_type=MESH)
     for load in loads:
         load.wait()
     near_copy.wait()
@@ -145,6 +150,7 @@
         fpt[cols, pl.ds(0, half)] = fp[pl.ds(0, half), cols].T
 
     embed(pl.ds(0, half), half)
+    pl.semaphore_wait(ready, len(steps))
     for r in range(0, half, T):
         diagonal(r, T)
         if r:
@@ -174,10 +180,10 @@
         dpre[rows, :] = (back * gate[rows, quarter]).astype(BF16)
 
     x_copies, y_copies = [], []
-    span = NZ // 2
+    span = NZ // PARTS
     own = gy.shape[3]
-    for i in range(2):
-        rows = pl.ds(i * d_in // 2, d_in // 2)
+    for i in range(PARTS):
+        rows = pl.ds(i * d_in // PARTS, d_in // PARTS)
         part = dot_nn(fpt[rows, :], dpre[...]).astype(BF16)
         for k in range(span):
             zz = i * span + k
@@ -215,7 +221,7 @@
         return out
 
     more = []
-    for i in range(2):
+    for i in range(PARTS):
         y_copies[i].wait()
         zz = pl.ds(i * span, span)
         for xx in range(NX):
@@ -239,6 +245,26 @@
     for copy in x_copies:
         copy.start()
 
+    def level(zz):
+        return remote(
+            ky.at[zz], qky.at[z], s3.at[zz], t3.at[z], at(zz, x, y, c)
+        )
+
+    def arrival(zz):
+        return remote(
+            ky.at[zz], qky.at[zz], s3.at[zz], t3.at[zz], at(zz, x, y, c)
+        )
+
+    for i in range(PARTS):
+        for copy in y_copies[i * (NX - 1) : (i + 1) * (NX - 1)]:
+            copy.wait()
+        for zz in range(i * span, (i + 1) * span):
+            ky[zz] = total(hy[x, zz], qy[:, zz])
+
+            @pl.when(z != zz)
+            def _(zz=zz):
+                level(zz).start()
+
     for copy in z_copies:
         copy.wait()
     hz[...] = total(gz[z], rz).reshape(hz.shape)
@@ -247,16 +273,6 @@
         for k in (2, 1, 3)
     ]
     for copy in z_copies:
-        copy.start()
-
-    for copy in y_copies:
-        copy.wait()
-    ky[...] = total(hy[x], qy)
-    copies = [
-        remote(ky.at[(z + k) % NZ], qky.at[k - 1], s3.at[k - 1], t3.at[k - 1], z_peers[k - 1])
-        for k in (4, 3, 5, 2, 6, 1, 7)
-    ]
-    for copy in copies:
         copy.start()
 
     for copy in z_copies:
@@ -285,9 +301,17 @@
     x_copy.wait()
     f1[0] = kx[side] + r3x[...]
     last += spread(f1.at[0], r1.at[0], 1)
-    for copy in copies:
-        copy.wait()
-    f1[1] = total(ky[z], qky)
+    qky[z] = ky[z]
+    for zz in range(NZ):
+
+        @pl.when(z != zz)
+        def _(zz=zz):
+            arrival(zz).wait()
+
+    part = qky[0]
+    for zz in range(1, NZ):
+        part = part + qky[zz]
+    f1[1] = part
     last += spread(f1.at[1], r1.at[1], 2)
     for i in range(2):
         r1[i, blk] = f1[i]
@@ -347,34 +371,35 @@
             pltpu.VMEM((2, n1, 128), F32),
             pltpu.VMEM((n1, 128), F32),
             pltpu.VMEM((NZ, n1, 128), F32),
-            pltpu.VMEM((NZ - 1, n1, 128), F32),
+            pltpu.VMEM((NZ, n1, 128), F32),
             pltpu.VMEM((2, n2, c2), F32),
             pltpu.VMEM((n2, c2), F32),
             pltpu.VMEM((2, n1, 128), F32),
             pltpu.VMEM((2, 4, n1, 128), F32),
             pltpu.VMEM((n2, c2), F32),
             pltpu.VMEM((4, n2, c2), F32),
+            pltpu.SemaphoreType.REGULAR,
             dma((3,)),
             dma((pieces + 1,)),
             dma((pieces + 1,)),
             dma((pieces,)),
             dma((pieces,)),
-            dma((2, NX - 1)),
-            dma((2, NX - 1)),
-            dma((2,)),
-            dma((2,)),
+            dma((PARTS, NX - 1)),
+            dma((PARTS, NX - 1)),
+            dma((PARTS,)),
+            dma((PARTS,)),
             dma((NZ - 1,)),
             dma((NZ - 1,)),
             dma((NZ - 1,)),
             dma((NZ - 1,)),
-            dma((2, NX - 1)),
-            dma((2, NX - 1)),
+            dma((PARTS, NX - 1)),
+            dma((PARTS, NX - 1)),
             dma((NX - 1,)),
             dma((NX - 1,)),
             dma,
             dma,
-            dma((NZ - 1,)),
-            dma((NZ - 1,)),
+            dma((NZ,)),
+            dma((NZ,)),
             dma,
             dma,
             dma((3, 3)),

time: 82.9 us -> 85.1 us (1.027)
  Pallas kernels: 80.9 us -> 83.1 us
    pallas_call x1, Pallas kernels: 80.9 us -> 83.1 us  [gradients(): pl.pallas_call(functools.partial(step_kernel, scale), out_shape=(jax.Shap...]
where the time goes in v6:
time: 85.1 us; the launch traced here: 85 us
  Pallas kernels  83.1 us (98%)
  local copies, waits for them, and re-layouts  1.27 us (1%)
    pallas_call x1, Pallas kernels, gradients(): pl.pallas_call(functools.partial(step_kernel, scale), out_shape=(jax.Shap...  83.1 us

profile of v6, /device:TPU:1, one launch (start us, length us, event | category | flops | bytes accessed | tf_op | source)
XLA Modules:
  0.0 85.0 jit_solution(7405382770860259584)
XLA Ops:
  0.6 83.1 %gradients.1 = (f32[32,1024]{1,0:T(8,128)S(1)}, f32[16,512]{1,0:T(8,128)S(1)}) custom-call(bf16[384,2048]{1,0:T(8,128)(2,1)} %fp_in.1, bf16[2048,1024]{1,0:T(8,128)(2,1)} %w1_in.1, bf16[1024,512]{1,0:T(8,128)(2,1)} %w2_in.1), custom_call_target="tpu_custom_call" | custom-call | tf_op jit(solution)/shard_map/gradients/pallas_call | solution.py:337
  83.7 0.7 copy.7
  84.4 0.6 copy.8

commit v7 on v6

--- a/solution.py
+++ b/solution.py
@@ -13,8 +13,8 @@
 BF16 = jnp.bfloat16
 NZ, NX = 8, 4
 T = 256
-PARTS = 4
-SPLIT = (2, 2, 1, 1)
+PARTS = 2
+SPLIT = (3, 2, 1)
 
 
 def dot_nt(a, b):

time: 85.1 us -> 83 us (0.975)
  Pallas kernels: 83.1 us -> 81 us
    pallas_call x1, Pallas kernels: 83.1 us -> 81 us  [gradients(): pl.pallas_call(functools.partial(step_kernel, scale), out_shape=(jax.Shap...]
where the time goes in v7:
time: 83 us; the launch traced here: 82.9 us
  Pallas kernels  81 us (98%)
  local copies, waits for them, and re-layouts  1.27 us (2%)
    pallas_call x1, Pallas kernels, gradients(): pl.pallas_call(functools.partial(step_kernel, scale), out_shape=(jax.Shap...  81 us

profile of v7, /device:TPU:1, one launch (start us, length us, event | category | flops | bytes accessed | tf_op | source)
XLA Modules:
  0.0 82.9 jit_solution(16596762161529377190)
XLA Ops:
  0.6 81.0 %gradients.1 = (f32[32,1024]{1,0:T(8,128)S(1)}, f32[16,512]{1,0:T(8,128)S(1)}) custom-call(bf16[384,2048]{1,0:T(8,128)(2,1)} %fp_in.1, bf16[2048,1024]{1,0:T(8,128)(2,1)} %w1_in.1, bf16[1024,512]{1,0:T(8,128)(2,1)} %w2_in.1), custom_call_target="tpu_custom_call" | custom-call | tf_op jit(solution)/shard_map/gradients/pallas_call | solution.py:337
  81.6 0.7 copy.7
  82.3 0.6 copy.8

commit v8 on v7

--- a/solution.py
+++ b/solution.py
@@ -75,6 +75,12 @@
             device_id=peer, device_id_type=MESH,
         )
 
+    pending = []
+
+    def landed(copy):
+        copy.wait_recv()
+        pending.append(copy)
+
     def far_copy(p):
         return remote(
             fp_in.at[pl.ds(firsts[p], sizes[p])],
@@ -101,7 +107,7 @@
         pl.semaphore_signal(ready, inc=1, device_id=peer, device_id_type=MESH)
     for load in loads:
         load.wait()
-    near_copy.wait()
+    landed(near_copy)
 
     def encode_columns(rows, cols):
         pre = dot_nn(fp[rows, :], w1[:, cols])
@@ -159,9 +165,9 @@
     for p in range(pieces):
         first, count = half + 2 * firsts[p], 2 * sizes[p]
         rows = pl.ds(first, count)
-        far_copy(p).wait()
+        landed(far_copy(p))
         passing(p).start()
-        passing(p).wait()
+        landed(passing(p))
         for n in range(0, hidden, T):
             encode_columns(rows, pl.ds(n, T))
         for n in range(0, d_in, T):
@@ -222,7 +228,7 @@
 
     more = []
     for i in range(PARTS):
-        y_copies[i].wait()
+        landed(y_copies[i])
         zz = pl.ds(i * span, span)
         for xx in range(NX):
             hy[xx, zz] = (gy[side, zz, xx].astype(F32) + ry[zz, xx].astype(F32)).astype(BF16)
@@ -236,7 +242,7 @@
     y_copies = more
 
     for copy in x_copies:
-        copy.wait()
+        landed(copy)
     hx[...] = total(gx[x], rx).astype(BF16)
     x_copies = [
         remote(hx.at[(z + k) % NZ], qx.at[k - 1], xs2.at[k - 1], xr2.at[k - 1], z_peers[k - 1])
@@ -257,7 +263,7 @@
 
     for i in range(PARTS):
         for copy in y_copies[i * (NX - 1) : (i + 1) * (NX - 1)]:
-            copy.wait()
+            landed(copy)
         for zz in range(i * span, (i + 1) * span):
             ky[zz] = total(hy[x, zz], qy[:, zz])
 
@@ -266,7 +272,7 @@
                 level(zz).start()
 
     for copy in z_copies:
-        copy.wait()
+        landed(copy)
     hz[...] = total(gz[z], rz).reshape(hz.shape)
     z_copies = [
         remote(hz.at[(x + k) % NX], qz.at[k - 1], zs2.at[k - 1], zr2.at[k - 1], x_peers[k - 1])
@@ -276,16 +282,16 @@
         copy.start()
 
     for copy in z_copies:
-        copy.wait()
+        landed(copy)
     kz[...] = total(hz[x], qz).reshape(kz.shape)
     z_copy = remote(kz.at[1 - side], r3z, zs3, zr3, pair)
     z_copy.start()
     for copy in x_copies:
-        copy.wait()
+        landed(copy)
     kx[...] = total(hx[z], qx).reshape(kx.shape)
     x_copy = remote(kx.at[1 - side], r3x, xs3, xr3, pair)
     x_copy.start()
-    z_copy.wait()
+    landed(z_copy)
     f2[...] = kz[side] + r3z[...]
 
     def spread(src, dst, i):
@@ -298,7 +304,7 @@
         return out
 
     last = spread(f2, r2, 0)
-    x_copy.wait()
+    landed(x_copy)
     f1[0] = kx[side] + r3x[...]
     last += spread(f1.at[0], r1.at[0], 1)
     qky[z] = ky[z]
@@ -317,7 +323,9 @@
         r1[i, blk] = f1[i]
     r2[blk] = f2[...]
     for copy in last:
-        copy.wait()
+        landed(copy)
+    for copy in pending:
+        copy.wait_send()
     for q in range(4):
         for i in range(2):
             o1[:, (2 * q + i) * 128 : (2 * q + i + 1) * 128] = r1[i, q]

time: 83 us -> 82.5 us (level)
  no operation moved by 1% of the time
where the time goes in v8:
time: 82.5 us; the launch traced here: 82.4 us
  Pallas kernels  80.5 us (98%)
  local copies, waits for them, and re-layouts  1.27 us (2%)
    pallas_call x1, Pallas kernels, gradients(): pl.pallas_call(functools.partial(step_kernel, scale), out_shape=(jax.Shap...  80.5 us

profile of v8, /device:TPU:1, one launch (start us, length us, event | category | flops | bytes accessed | tf_op | source)
XLA Modules:
  0.0 82.4 jit_solution(11779729209545304452)
XLA Ops:
  0.6 80.5 %gradients.1 = (f32[32,1024]{1,0:T(8,128)S(1)}, f32[16,512]{1,0:T(8,128)S(1)}) custom-call(bf16[384,2048]{1,0:T(8,128)(2,1)} %fp_in.1, bf16[2048,1024]{1,0:T(8,128)(2,1)} %w1_in.1, bf16[1024,512]{1,0:T(8,128)(2,1)} %w2_in.1), custom_call_target="tpu_custom_call" | custom-call | tf_op jit(solution)/shard_map/gradients/pallas_call | solution.py:345
  81.1 0.7 copy.7
  81.8 0.6 copy.8

commit v9 on v8

--- a/solution.py
+++ b/solution.py
@@ -178,11 +178,12 @@
         if p:
             cross(pl.ds(half, first - half), rows)
 
-    demb[...] = (summed[...] * scale).astype(BF16)
     quarter = pl.ds(pl.multiple_of(blk * T, T), T)
     for r in range(0, rows_all, 2 * T):
         rows = pl.ds(r, 2 * T)
-        back = dot_nt(demb[rows, :], w2[quarter, :])
+        part = (summed[rows, :] * scale).astype(BF16)
+        demb[rows, :] = part
+        back = dot_nt(part, w2[quarter, :])
         dpre[rows, :] = (back * gate[rows, quarter]).astype(BF16)
 
     x_copies, y_copies = [], []

time: 82.5 us -> 82.6 us (level)
  no operation moved by 1% of the time
where the time goes in v9:
time: 82.6 us; the launch traced here: 82.5 us
  Pallas kernels  80.6 us (98%)
  local copies, waits for them, and re-layouts  1.27 us (2%)
    pallas_call x1, Pallas kernels, gradients(): pl.pallas_call(functools.partial(step_kernel, scale), out_shape=(jax.Shap...  80.6 us

profile of v9, /device:TPU:1, one launch (start us, length us, event | category | flops | bytes accessed | tf_op | source)
XLA Modules:
  0.0 82.5 jit_solution(10111137871002883922)
XLA Ops:
  0.6 80.6 %gradients.1 = (f32[32,1024]{1,0:T(8,128)S(1)}, f32[16,512]{1,0:T(8,128)S(1)}) custom-call(bf16[384,2048]{1,0:T(8,128)(2,1)} %fp_in.1, bf16[2048,1024]{1,0:T(8,128)(2,1)} %w1_in.1, bf16[1024,512]{1,0:T(8,128)(2,1)} %w2_in.1), custom_call_target="tpu_custom_call" | custom-call | tf_op jit(solution)/shard_map/gradients/pallas_call | solution.py:346
  81.2 0.7 copy.7
  81.9 0.6 copy.8
